TPU v7x, 32 devices: a whole 2x2x4 slice. The times are simulated.
32 devices in a mesh: grp: 2 (over x), seq: 16 (over z, y, core).
Axes of the slice: x: 2, y: 2, z: 4, core: 2. Of those that a mesh axis runs over, the one named last changes fastest.
Arguments:
- hidden: bfloat16 [4, 5120, 1280], P('grp', 'seq'), parts along dimension 0, may hold values from -160 to 160
- mod_shift: float32 [5120], replicated, may hold values from -3 to 3
- mod_scale: float32 [5120], replicated, may hold values from -0.5 to 0.5
- head_weight: float32 [64, 5120], replicated, may hold values from -0.078125 to 0.078125
- head_bias: float32 [64], replicated, may hold values from -3 to 3
- conv_in_weight: bfloat16 [3, 3, 3, 16, 384], replicated, may hold values from -0.3125 to 0.3125
- conv_in_bias: float32 [384], replicated, may hold values from -3 to 3
- gain_in: float32 [384], replicated, may hold values from 0.1 to 1.9
- up_weight: bfloat16 [3, 3, 384, 192], replicated, may hold values from -0.109375 to 0.109375
- up_bias: float32 [192], replicated, may hold values from -3 to 3
- gain_up: float32 [192], replicated, may hold values from 0.1 to 1.9
- out_weight: bfloat16 [3, 3, 3, 192, 96], replicated, may hold values from -0.078125 to 0.078125
- out_bias: float32 [96], replicated, may hold values from -2 to 2
Outputs:
- decoded: bfloat16 [4, 64, 320, 96], P('grp', 'seq'), parts along dimension 0
There are 2 independent parts, one for each index of `grp`. A program takes and returns all parts, laid end to end along the dimension named above; an argument that names none is the same for every part. Nothing has to cross between parts.
All inputs are finite; a program needn't handle non-finite values.
Results may differ from a plain program's by a relative error of at most 0.0056.
Values may be sent and summed in bfloat16 or wider, within the bound.
A program may use at most 64 MiB of HBM per device.

v0:
```python
import jax
import jax.numpy as jnp
from jax import lax
from jax.sharding import PartitionSpec as P

TOK_W = 80


def padded_2(block, sides, width):
    for axis, dim in sides:
        count = lax.axis_size(axis)
        forward = [(i, i + 1) for i in range(count - 1)]
        backward = [(target, source) for source, target in forward]
        low = lax.ppermute(
            lax.slice_in_dim(block, block.shape[dim] - width, None, axis=dim), axis, forward
        )
        high = lax.ppermute(lax.slice_in_dim(block, 0, width, axis=dim), axis, backward)
        block = jnp.concatenate([low, block, high], axis=dim)
    return block


def rms_silu(values, gain_vec):
    squares = jnp.mean(values * values, axis=-1, keepdims=True)
    normed = values * lax.rsqrt(squares + 1e-06) * gain_vec
    return normed * jax.nn.sigmoid(normed)


def conv_time(values, weight):
    padded = jnp.pad(values, ((2, 0), (0, 0), (1, 1), (0, 0)))
    result = lax.conv_general_dilated(
        padded[None],
        weight,
        (1, 1, 1),
        "VALID",
        dimension_numbers=("NDHWC", "DHWIO", "NDHWC"),
        preferred_element_type=jnp.float32,
    )
    return result[0]


def conv_plane(values, weight):
    padded = jnp.pad(values, ((0, 0), (0, 0), (1, 1), (0, 0)))
    return lax.conv_general_dilated(
        padded,
        weight,
        (1, 1),
        "VALID",
        dimension_numbers=("NHWC", "HWIO", "NHWC"),
        preferred_element_type=jnp.float32,
    )


def double_grid(values):
    return jnp.repeat(jnp.repeat(values, 2, axis=1), 2, axis=2)


def keep_rows(values, first_row, total_rows):
    grid_row = first_row + jnp.arange(values.shape[1], dtype=jnp.int32)
    inside = (grid_row >= 0) & (grid_row < total_rows)
    return jnp.where(inside[None, :, None, None], values, 0.0)


def local(
    hidden,
    mod_shift,
    mod_scale,
    head_weight,
    head_bias,
    conv_in_weight,
    conv_in_bias,
    gain_in,
    up_weight,
    up_bias,
    gain_up,
    out_weight,
    out_bias,
):
    num_dev = lax.axis_size("seq")
    dev_index = lax.axis_index("seq")
    frames, feat_local, tok_total = hidden.shape
    tok_cols = TOK_W
    rows_dev = tok_total // tok_cols // num_dev
    patch_len = head_weight.shape[0]
    lat_ch = patch_len // 4
    tokens_tile = lax.all_to_all(hidden, "seq", split_axis=2, concat_axis=1, tiled=True)
    values = tokens_tile.astype(jnp.float32)
    token_mean = jnp.mean(values, axis=1, keepdims=True)
    centred = values - token_mean
    variance = jnp.mean(centred * centred, axis=1, keepdims=True)
    modded = centred * lax.rsqrt(variance + 1e-06) * (1.0 + mod_scale)[:, None] + mod_shift[:, None]
    projected = (
        jnp.einsum("fdt,kd->ftk", modded, head_weight, precision=lax.Precision.HIGHEST) + head_bias
    )
    grid = projected.astype(jnp.bfloat16).reshape(frames, rows_dev, tok_cols, 2, 2, lat_ch)
    lat_rows = 2 * rows_dev
    lat_cols = 2 * tok_cols
    latent = grid.transpose(0, 1, 3, 2, 4, 5).reshape(frames, lat_rows, lat_cols, lat_ch)
    latent_ext = padded_2(latent.reshape(frames, lat_rows, lat_cols * lat_ch), (("seq", 1),), 2)
    latent_ext = latent_ext.reshape(frames, lat_rows + 4, lat_cols, lat_ch)
    first_pre = rms_silu(conv_time(latent_ext, conv_in_weight) + conv_in_bias, gain_in)
    first_act = keep_rows(first_pre, dev_index * lat_rows - 1, lat_rows * num_dev).astype(
        jnp.bfloat16
    )
    upsampled = double_grid(first_act)
    second_pre = rms_silu(conv_plane(upsampled, up_weight) + up_bias, gain_up)
    second_ext = keep_rows(second_pre, 2 * dev_index * lat_rows - 1, 2 * lat_rows * num_dev).astype(
        jnp.bfloat16
    )
    return (conv_time(second_ext, out_weight) + out_bias).astype(jnp.bfloat16)


def solution(mesh):
    placed = (P("grp", "seq", None), P(), P(), P(), P(), P(), P(), P(), P(), P(), P(), P(), P())
    return jax.shard_map(
        local, mesh=mesh, in_specs=placed, out_specs=P("grp", "seq", None, None), check_vma=False
    )
```

profile of v0, /device:TPU:13, one launch (start us, length us, event | category | flops | bytes accessed | tf_op | source)
XLA Modules:
  0.0 136.1 jit_solution(6802326855571328485)
XLA Ops:
  0.0 0.0 copy-start
  0.0 6.7 %copy.79 = bf16[2,320,1280]{1,0,2:T(2,128)(2,1)} copy(bf16[2,320,1280]{2,1,0:T(8,128)(2,1)} %param.13) | data formatting | bytes 3276800 | tf_op args[0]
  6.8 6.5 %all-to-all-start = ((bf16[2,320,1280]{1,0,2:T(2,128)(2,1)}), bf16[2,320,1280]{1,0,2:T(2,128)(2,1)S(1)}, u32[]{:S(2)}, u32[]{:S(2)}) async-start(bf16[2,320,1280]{1,0,2:T(2,128)(2,1)} %copy.79), calls=%async_computation | async-start | bytes 3932160 | tf_op jit(solution)/shard_map/all_to_all | solution.py:85
  13.3 0.0 copy-done.4
  13.3 44.6 %all-to-all-done = bf16[2,320,1280]{1,0,2:T(2,128)(2,1)S(1)} async-done(((bf16[2,320,1280]{1,0,2:T(2,128)(2,1)}), bf16[2,320,1280]{1,0,2:T(2,128)(2,1)S(1)}, u32[]{:S(2)}, u32[]{:S(2)}) %all-to-all-start) | async-done | bytes 1638432 | tf_op jit(solution)/shard_map/all_to_all | solution.py:85
  57.9 0.3 copy.80
  58.1 0.4 fusion.22
  58.6 0.3 convert_bitcast_fusion
  58.8 0.7 multiply_reduce_fusion.1
  59.6 3.0 %copy.81 = f32[2,16,320,80]{2,1,3,0:T(8,128)} copy(f32[2,16,320,80]{2,3,1,0:T(8,128)S(1)} %convert_bitcast_fusion) | data formatting | bytes 6553600 | tf_op jit(solution)/shard_map/convert_element_type | solution.py:86
  62.6 5.2 %reshape.96 = f32[2,5120,80]{1,2,0:T(8,128)} reshape(f32[2,16,320,80]{2,1,3,0:T(8,128)} %copy.81) | data formatting | bytes 6553600 | tf_op jit(solution)/shard_map/convert_element_type | solution.py:86
  67.8 0.0 copy-done.2
  67.8 0.0 copy-done.3
  67.8 0.0 copy-done.8
  67.8 6.1 %fusion.47 = bf16[2,80,64]{1,2,0:T(8,128)(2,1)S(1)} fusion(f32[64,5120]{1,0:T(8,128)S(1)} %copy-done.2, f32[2,5120,80]{1,2,0:T(8,128)} %reshape.96, f32[5120]{0:T(1024)S(1)} %copy-done.3, f32[5120]{0:T(1024)S(1)} %broadcast_add_fusion, f32[2,80]{1,0:T(2,128)S(1)} %add_rsqrt_fusion.2, f32[2,80]{1,0:T(2,128)S(1)} %broadcast_multiply_fusion, f32[64]{0:T(128)S(1)} %copy-done.8), kind=kOutput, calls=%fused_computation.53 | convolution fusion | flops 632442880 | bytes 4650496 | tf_op jit(solution)/shard_map/fdt,kd->ftk/dot_general | solution.py:92
  74.0 0.1 copy.82
  74.1 0.2 reshape_reshape.3
  74.3 2.0 %collective-permute-start.1 = (bf16[2,2,2560]{2,1,0:T(2,128)(2,1)S(1)}, bf16[2,2,2560]{2,1,0:T(2,128)(2,1)S(1)}, u32[]{:S(2)}, u32[]{:S(2)}) collective-permute-start(bf16[2,2,2560]{2,1,0:T(2,128)(2,1)S(1)} %reshape_reshape.3), channel_id=1, source_target_pairs={{1,0},{2,1},{3,2},{4,3},{5,4},{6,5},{7,6},{8,7},{9,8},{10,9},{11,1... | collective-permute-start | bytes 61448 | tf_op jit(solution)/shard_map/ppermute | solution.py:17
  76.3 4.6 %collective-permute-start = (bf16[2,2,2560]{2,1,0:T(2,128)(2,1)S(1)}, bf16[2,2,2560]{2,1,0:T(2,128)(2,1)S(1)}, u32[]{:S(2)}, u32[]{:S(2)}) collective-permute-start(bf16[2,2,2560]{2,1,0:T(2,128)(2,1)S(1)} %reshape_reshape.3), channel_id=1, source_target_pairs={{0,1},{1,2},{2,3},{3,4},{4,5},{5,6},{6,7},{7,8},{8,9},{9,10},{10,1... | collective-permute-start | bytes 61448 | tf_op jit(solution)/shard_map/ppermute | solution.py:14
  81.0 0.1 copy.84
  81.1 0.6 collective-permute-done
  81.6 0.2 concatenate.10
  81.8 0.1 copy.83
  81.9 0.0 collective-permute-done.1
  81.9 0.2 concatenate.12
  82.1 0.1 copy.85
  82.2 0.1 fusion.61
  82.4 0.6 reshape.75
  83.0 1.6 %copy.87 = bf16[4,6,1,8,21,16]{5,3,4,1,0,2:T(8,128)(2,1)S(1)} copy(bf16[4,6,1,8,21,16]{4,3,5,1,0,2:T(8,128)(2,1)S(1)} %reshape.75) | data formatting | bytes 258048 | tf_op jit(solution)/shard_map/conv_general_dilated | solution.py:30
  84.6 0.0 copy-done.14
  84.6 2.6 %convolution_select_fusion = f32[2,4,8,21,384]{4,2,3,1,0:T(8,128)S(1)} fusion(bf16[3,3,3,16,384]{4,3,2,1,0:T(8,128)(2,1)} %param.18, bf16[4,6,1,7,2,16]{5,3,4,1,0,2:T(8,128)(2,1)S(1)} %slice.7, bf16[4,6,1,8,21,16]{5,3,4,1,0,2:T(8,128)(2,1)S(1)} %copy.87, pred[8,21]{0,1:T(8,128)(4,1)S(1)} %copy-done.14), kind=kOutput, calls=%fused_computation.41 | convolution fusion | flops 446846976 | bytes 2536104 | tf_op jit(solution)/shard_map/conv_general_dilated | solution.py:30
  87.2 0.0 copy-start.5
  87.2 0.0 copy-start.6
  87.2 0.5 copy.88
  87.7 0.1 copy-done.5
  87.8 0.6 multiply_reduce_fusion.2
  88.5 1.5 %select_convert_fusion.1 = bf16[2,4,160,384]{3,1,2,0:T(4,128)(2,1)S(1)} fusion(f32[2,4,1,168,384]{4,1,3,0,2:T(4,128)S(1)} %bitcast.88, f32[384]{0:T(512)S(1)} %copy-done.6, f32[2,4,160]{1,2,0:T(8,128)S(1)} %add_rsqrt_fusion, f32[384]{0:T(512)S(1)} %copy-done.5, pred[4]{0:T(512)(128)(4,1)S(1)} %compare_and_fusion), kind=kLoop, calls=%fused_computation.35 | loop fusion | flops 4423680 | bytes 2957316 | tf_op jit(solution)/shard_map/convert_element_type | solution.py:101
  89.9 1.4 broadcast_in_dim.52
  91.3 1.8 %reshape.71 = bf16[2,8,160,384]{3,1,2,0:T(8,128)(2,1)} reshape(bf16[2,4,2,160,384]{4,2,1,3,0:T(2,128)(2,1)S(1)} %broadcast_in_dim.52) | data formatting | bytes 3932160 | tf_op jit(solution)/shard_map/reshape | solution.py:54
  93.1 1.9 %broadcast_in_dim.53 = bf16[2,8,160,2,384]{4,1,3,2,0:T(8,128)(2,1)S(1)} broadcast(bf16[2,8,160,384]{3,1,2,0:T(8,128)(2,1)} %reshape.71), dimensions={0,1,2,4} | broadcast | bytes 5898240 | tf_op jit(solution)/shard_map/broadcast_in_dim | solution.py:54
  95.0 0.4 pad.14
  95.4 0.0 copy-start.11
  95.4 0.0 copy-start.13
  95.4 0.5 fusion.6
  95.9 0.2 copy-done.11
  96.1 0.0 copy-done.13
  96.1 9.7 %multiply_reduce_fusion = (f32[6,16,41]{1,2,0:T(8,128)S(1)}, f32[6,16,41,192]{3,1,2,0:T(8,128)}) fusion(f32[192]{0:T(256)S(1)} %copy-done.11, bf16[3,3,384,192]{2,3,1,0:T(8,128)(2,1)S(1)} %copy-done, bf16[8,2,8,43,384]{4,0,3,2,1:T(8,128)(2,1)S(1)} %fusion.6, pred[16,41]{0,1:T(8,128)(4,1)S(1)} %copy-done.13), kind=kOutput, calls=%fused_computation.14 | convolution fusion | flops 5226500096 | bytes 8594192 | tf_op jit(solution)/shard_map/conv_general_dilated | solution.py:43
  105.8 0.1 copy.93
  105.9 0.1 reshape.88
  106.1 6.6 %copy.92 = f32[6,16,41,192]{3,2,1,0:T(8,128)} copy(f32[6,16,41,192]{3,1,2,0:T(8,128)} %get-tuple-element.6) | data formatting | bytes 6045696 | tf_op jit(solution)/shard_map/add | solution.py:105
  112.7 5.0 %reshape.86 = f32[6,2,328,192]{3,2,1,0:T(8,128)} reshape(f32[6,16,41,192]{3,2,1,0:T(8,128)} %copy.92) | data formatting | bytes 6045696 | tf_op jit(solution)/shard_map/add | solution.py:105
  117.7 3.1 %select_convert_fusion = bf16[2,6,320,192]{3,2,0,1:T(8,128)(2,1)S(1)} fusion(f32[6,2,328,192]{3,2,1,0:T(8,128)} %reshape.86, f32[192]{0:T(256)S(1)} %copy-done.7, f32[2,6,320]{2,0,1:T(2,128)S(1)} %slice_bitcast_fusion.3, pred[6]{0:T(512)(128)(4,1)S(1)} %compare_and_fusion.1), kind=kLoop, calls=%fused_computation.21 | loop fusion | flops 5898240 | bytes 4439814 | tf_op jit(solution)/shard_map/convert_element_type | solution.py:106
  120.8 0.7 pad_bitcast_fusion
  121.5 1.5 %copy.99 = bf16[4,6,1,322,192]{4,0,3,1,2:T(4,128)(2,1)S(1)} copy(bf16[4,6,1,322,192]{4,3,0,1,2:T(8,128)(2,1)S(1)} %pad_bitcast_fusion) | data formatting | bytes 5935104
  123.1 1.8 %pad.16.clone = bf16[4,6,1,328,192]{4,0,3,1,2:T(4,128)(2,1)S(1)} pad(bf16[4,6,1,322,192]{4,0,3,1,2:T(4,128)(2,1)S(1)} %copy.99, bf16[]{:T(256)} %constant.39.clone.1), padding=0_0x0_0x0_0x0_6x0_0 | pad | bytes 5990402 | tf_op jit(solution)/shard_map/broadcast_in_dim | solution.py:31
  124.9 0.0 copy-start.10
  124.9 0.0 copy-start.12
  124.9 0.5 copy.96
  125.5 0.7 copy-done.10
  126.2 8.1 %fusion.30 = f32[2,4,8,41,96]{4,2,3,1,0:T(8,128)S(1)} fusion(bf16[3,3,3,192,96]{4,3,2,1,0:T(8,128)(2,1)S(1)} %copy-done.10, bf16[4,6,1,7,2,192]{5,3,4,1,0,2:T(8,128)(2,1)S(1)} %slice.12, bf16[4,6,1,8,41,192]{5,3,4,1,0,2:T(8,128)(2,1)S(1)} %copy.96, pred[8,41]{0,1:T(8,128)(4,1)S(1)} %copy-done.12), kind=kOutput, calls=%fused_computation.42 | convolution fusion | flops 2621503488 | bytes 5155144 | tf_op jit(solution)/shard_map/conv_general_dilated | solution.py:30
  134.3 0.3 copy.97
  134.7 0.2 fusion.34
  134.9 1.2 copy.98
  136.1 0.0 copy-done.1
  (25 shorter events, 0.2 us)
Async XLA Ops:
  0.0 95.9 %copy-start = (bf16[3,3,384,192]{2,3,1,0:T(8,128)(2,1)S(1)}, bf16[3,3,384,192]{2,3,1,0:T(8,128)(2,1)}, u32[]{:S(2)}) copy-start(bf16[3,3,384,192]{2,3,1,0:T(8,128)(2,1)} %param.21) | copy-start | bytes 3981316
  0.0 13.3 %copy-start.4 = (f32[5120]{0:T(1024)S(1)}, f32[5120]{0:T(1024)}, u32[]{:S(2)}) copy-start(f32[5120]{0:T(1024)} %param.15) | copy-start | bytes 61444
  6.8 51.1 %all-to-all-start = ((bf16[2,320,1280]{1,0,2:T(2,128)(2,1)}), bf16[2,320,1280]{1,0,2:T(2,128)(2,1)S(1)}, u32[]{:S(2)}, u32[]{:S(2)}) async-start(bf16[2,320,1280]{1,0,2:T(2,128)(2,1)} %copy.79), calls=%async_computation | async-start | bytes 3932160 | tf_op jit(solution)/shard_map/all_to_all | solution.py:85
  62.6 5.2 %copy-start.2 = (f32[64,5120]{1,0:T(8,128)S(1)}, f32[64,5120]{1,0:T(8,128)}, u32[]{:S(2)}) copy-start(f32[64,5120]{1,0:T(8,128)} %param.16) | copy-start | bytes 3932164
  62.6 5.2 %copy-start.3 = (f32[5120]{0:T(1024)S(1)}, f32[5120]{0:T(1024)}, u32[]{:S(2)}) copy-start(f32[5120]{0:T(1024)} %param.14) | copy-start | bytes 61444
  62.6 5.2 %copy-start.8 = (f32[64]{0:T(128)S(1)}, f32[64]{0:T(128)}, u32[]{:S(2)}) copy-start(f32[64]{0:T(128)} %param.17) | copy-start | bytes 772
  73.9 10.6 %copy-start.14 = (pred[8,21]{0,1:T(8,128)(4,1)S(1)}, pred[8,21]{0,1:T(8,128)(4,1)}, u32[]{:S(2)}) copy-start(pred[8,21]{0,1:T(8,128)(4,1)} %constant.60) | copy-start | bytes 508
  74.3 7.6 %collective-permute-start.1 = (bf16[2,2,2560]{2,1,0:T(2,128)(2,1)S(1)}, bf16[2,2,2560]{2,1,0:T(2,128)(2,1)S(1)}, u32[]{:S(2)}, u32[]{:S(2)}) collective-permute-start(bf16[2,2,2560]{2,1,0:T(2,128)(2,1)S(1)} %reshape_reshape.3), channel_id=1, source_target_pairs={{1,0},{2,1},{3,2},{4,3},{5,4},{6,5},{7,6},{8,7},{9,8},{10,9},{11,1... | collective-permute-start | bytes 61448 | tf_op jit(solution)/shard_map/ppermute | solution.py:17
  76.3 5.3 %collective-permute-start = (bf16[2,2,2560]{2,1,0:T(2,128)(2,1)S(1)}, bf16[2,2,2560]{2,1,0:T(2,128)(2,1)S(1)}, u32[]{:S(2)}, u32[]{:S(2)}) collective-permute-start(bf16[2,2,2560]{2,1,0:T(2,128)(2,1)S(1)} %reshape_reshape.3), channel_id=1, source_target_pairs={{0,1},{1,2},{2,3},{3,4},{4,5},{5,6},{6,7},{7,8},{8,9},{9,10},{10,1... | collective-permute-start | bytes 61448 | tf_op jit(solution)/shard_map/ppermute | solution.py:14
  87.2 0.7 copy-start.5
  87.2 1.3 copy-start.6
  95.4 0.7 copy-start.11
  95.4 0.7 copy-start.13
  112.7 5.0 %copy-start.7 = (f32[192]{0:T(256)S(1)}, f32[192]{0:T(256)}, u32[]{:S(2)}) copy-start(f32[192]{0:T(256)} %param.23) | copy-start | bytes 2308
  124.9 1.3 copy-start.10
  124.9 1.3 copy-start.12
  126.2 8.5 %copy-start.9 = (f32[96]{0:T(128)S(1)}, f32[96]{0:T(128)}, u32[]{:S(2)}) copy-start(f32[96]{0:T(128)} %param.25) | copy-start | bytes 1156
  126.2 9.9 %copy-start.1 = (bf16[3,3,384,192]{2,3,1,0:T(8,128)(2,1)S(1)}, bf16[3,3,384,192]{2,3,1,0:T(8,128)(2,1)}, u32[]{:S(2)}) copy-start(bf16[3,3,384,192]{2,3,1,0:T(8,128)(2,1)} %param.21) | copy-start | bytes 3981316
where the time goes:
time: 138 us; the launch traced here: 136 us
  waiting for transfers between devices  45.2 us (33%)
  local copies, waits for them, and re-layouts  43.5 us (32%)
  matrix products  26.5 us (19%)
  starting transfers between devices  13.2 us (10%)
  other arithmetic  7.41 us (5%)
    all_to_all x1, waiting for transfers between devices, local(): lax.all_to_all(hidden, 'seq', split_axis=2, concat_axis=1, tiled=True)  44.6 us
    add x2, local copies, waits for them, and re-layouts, local(): second_pre = rms_silu(conv_plane(upsampled, up_weight) + up_bias, gain_up)  11.6 us
    conv_general_dilated x2, matrix products, conv_time(): lax.conv_general_dilated(padded[None], weight, (1, 1, 1), 'VALID', dimens...  10.7 us
    conv_general_dilated x1, matrix products, conv_plane(): lax.conv_general_dilated(padded, weight, (1, 1), 'VALID', dimension_numbe...  9.71 us
    unnamed x33, local copies, waits for them, and re-layouts  9.48 us
    convert_element_type x2, local copies, waits for them, and re-layouts, local(): values = tokens_tile.astype(jnp.float32)  8.24 us
    all_to_all x1, starting transfers between devices, local(): lax.all_to_all(hidden, 'seq', split_axis=2, concat_axis=1, tiled=True)  6.52 us
    dot_general x1, matrix products, local(): jnp.einsum('fdt,kd->ftk', modded, head_weight, precision=lax.Precision.HI...  6.11 us
  transfers between devices with their start and end apart: 3, of which 2 were waited for; matrix products, arithmetic and copies ran while one was open for 0% of the time, Pallas kernels for 0%

commit v1 on v0

v1 whole, which is shorter than its diff:
```python
import functools

import jax
import jax.numpy as jnp
from jax import lax
from jax.experimental import pallas as pl
from jax.experimental.pallas import tpu as pltpu
from jax.sharding import PartitionSpec as P

TOK_W = 80
HIGH = lax.Precision.HIGHEST
F32 = jnp.float32
BF16 = jnp.bfloat16


def rms_silu(values, gain_vec):
    squares = jnp.mean(values * values, axis=-1, keepdims=True)
    normed = values * lax.rsqrt(squares + 1e-06) * gain_vec
    return normed * jax.nn.sigmoid(normed)


def shift_cols(values, step):
    count = values.shape[0]
    col = lax.broadcasted_iota(jnp.int32, (count, 1), 0) % TOK_W
    if step > 0:
        return jnp.where(col == 0, 0.0, pltpu.roll(values, 1, 0))
    return jnp.where(col == TOK_W - 1, 0.0, pltpu.roll(values, count - 1, 0))


def conv_kernel(num_dev, lat_rows, chans, pos_ref, x_ref, w1_ref, b1_ref, g1_ref, w2_ref, b2_ref, g2_ref,
                w3_ref, b3_ref, out_ref, act1, act2, res):
    c1, c2, c3 = chans
    dev = pos_ref[0]
    rows1 = lat_rows + 2
    m1 = rows1 * TOK_W
    rows2 = lat_rows + 1
    m2 = rows2 * TOK_W
    rows3 = 2 * lat_rows
    m3 = rows3 * TOK_W

    def inside(count, first, step, total):
        row = lax.broadcasted_iota(jnp.int32, (count, 1), 0) // TOK_W * step + first
        return (row >= 0) & (row < total)

    keep1 = inside(m1, dev * lat_rows - 1, 1, num_dev * lat_rows)
    for frame in range(2):
        x_now = x_ref[frame].reshape(m1, x_ref.shape[-1])
        pre = jnp.dot(x_now, w1_ref[1], preferred_element_type=F32)
        if frame == 1:
            x_old = x_ref[0].reshape(m1, x_ref.shape[-1])
            pre = pre + jnp.dot(x_old, w1_ref[0], preferred_element_type=F32)
        for r in range(2):
            val = rms_silu(pre[:, r * c1 : (r + 1) * c1] + b1_ref[...], g1_ref[...])
            val = jnp.where(keep1, val, 0.0)
            edge = shift_cols(val, 1) if r == 1 else shift_cols(val, -1)
            spot = 0 if r == 1 else 3
            act1[frame, :, :, (r + 1) * c1 : (r + 2) * c1] = val.astype(BF16).reshape(rows1, TOK_W, c1)
            act1[frame, :, :, spot * c1 : (spot + 1) * c1] = edge.astype(BF16).reshape(rows1, TOK_W, c1)

    start = (0, 1, 1, 2)
    for p in range(2):
        first = 0 if p == 0 else -1
        keep2 = inside(m2, 2 * dev * lat_rows + first, 2, 2 * num_dev * lat_rows)
        for frame in range(2):
            for s in range(4):
                q = s % 2
                lanes = slice(start[s] * c1, (start[s] + 2) * c1)
                top = act1[frame, 0:rows2, :, lanes].reshape(m2, 2 * c1)
                low = act1[frame, 1 : rows2 + 1, :, lanes].reshape(m2, 2 * c1)
                pre = jnp.dot(top, w2_ref[p, 0, q], preferred_element_type=F32)
                pre = pre + jnp.dot(low, w2_ref[p, 1, q], preferred_element_type=F32)
                val = rms_silu(pre + b2_ref[...], g2_ref[...])
                val = jnp.where(keep2, val, 0.0)
                val = jnp.concatenate([val, jnp.zeros((m2, 256 - c2), F32)], axis=1)
                pieces = [(s + 1, val)]
                if s == 3:
                    pieces.append((0, shift_cols(val, 1)))
                if s == 0:
                    pieces.append((5, shift_cols(val, -1)))
                for spot, piece in pieces:
                    piece = piece.astype(BF16).reshape(rows2, TOK_W, 256)
                    for i in range(rows2):
                        act2[frame, 2 * i + 1 - p, :, spot * 256 : (spot + 1) * 256] = piece[i]

    for s in range(4):
        lanes = slice(s * 256, (s + 3) * 256)
        old = None
        new = None
        for b in range(3):
            before = act2[0, b : b + rows3, :, lanes].reshape(m3, 768)
            after = act2[1, b : b + rows3, :, lanes].reshape(m3, 768)
            one = jnp.dot(before, w3_ref[b], preferred_element_type=F32)
            two = jnp.dot(after, w3_ref[b, :, 0:128], preferred_element_type=F32)
            old = one if old is None else old + one
            new = two if new is None else new + two
        res[pl.ds(s, m3, stride=4), :] = old[:, 0:128] + b3_ref[...]
        res[pl.ds(4 * m3 + s, m3, stride=4), :] = old[:, 128:256] + new + b3_ref[...]
    out_ref[...] = res[:, 0:c3].astype(BF16)


def decode(x1, dev_index, num_dev, conv_in_weight, conv_in_bias, gain_in, up_weight, up_bias, gain_up, out_weight, out_bias):
    frames, rows1, cols, _ = x1.shape
    lat_rows = rows1 - 2
    lat_ch, c1 = conv_in_weight.shape[3:]
    c2, c3 = out_weight.shape[3:]
    taps = conv_in_weight[1:]
    none = jnp.zeros_like(taps[:, :, :1])
    w1 = jnp.stack(
        [jnp.concatenate([taps, none], axis=2), jnp.concatenate([none, taps], axis=2)], axis=4
    ).reshape(2, 12 * lat_ch, 2 * c1)
    wide = up_weight.astype(F32)
    by_row = jnp.stack(
        [jnp.stack([wide[0], wide[1] + wide[2]]), jnp.stack([wide[0] + wide[1], wide[2]])]
    )
    by_col = jnp.stack(
        [
            jnp.stack([by_row[:, :, 0], by_row[:, :, 1] + by_row[:, :, 2]], axis=2),
            jnp.stack([by_row[:, :, 0] + by_row[:, :, 1], by_row[:, :, 2]], axis=2),
        ],
        axis=2,
    )
    w2 = by_col.astype(BF16).reshape(2, 2, 2, 2 * c1, c2)
    w3 = jnp.pad(out_weight[1:], ((0, 0), (0, 0), (0, 0), (0, 256 - c2), (0, 128 - c3)))
    w3 = jnp.concatenate([w3[1], w3[0]], axis=-1).reshape(3, 768, 256)
    b3 = jnp.pad(out_bias, (0, 128 - c3))[None]
    cells = frames * 2 * lat_rows * 4 * cols
    vmem = pl.BlockSpec(memory_space=pltpu.VMEM)
    out = pl.pallas_call(
        functools.partial(conv_kernel, num_dev, lat_rows, (c1, c2, c3)),
        out_shape=jax.ShapeDtypeStruct((cells, c3), BF16),
        in_specs=[pl.BlockSpec(memory_space=pltpu.SMEM)] + [vmem] * 9,
        out_specs=vmem,
        scratch_shapes=[
            pltpu.VMEM((frames, rows1, cols, 4 * c1), BF16),
            pltpu.VMEM((frames, 2 * lat_rows + 2, cols, 6 * 256), BF16),
            pltpu.VMEM((cells, 128), F32),
        ],
        compiler_params=pltpu.CompilerParams(vmem_limit_bytes=40 * 1024 * 1024),
    )(dev_index[None].astype(jnp.int32), x1, w1, conv_in_bias[None], gain_in[None], w2, up_bias[None], gain_up[None], w3, b3)
    return out.reshape(frames, 2 * lat_rows, 4 * cols, c3)


def split3(weight):
    high = lax.reduce_precision(weight, 8, 7)
    rest = weight - high
    mid = lax.reduce_precision(rest, 8, 7)
    return jnp.concatenate([high.astype(BF16), mid.astype(BF16), (rest - mid).astype(BF16)], axis=0)


def local(
    hidden, mod_shift, mod_scale, head_weight, head_bias, conv_in_weight, conv_in_bias, gain_in,
    up_weight, up_bias, gain_up, out_weight, out_bias,
):
    num_dev = lax.axis_size("seq")
    dev_index = lax.axis_index("seq")
    frames, feat, tok_total = hidden.shape
    tile = tok_total // num_dev
    rows_dev = tile // TOK_W
    patch = head_weight.shape[0]
    lat_ch = patch // 4
    scaled = head_weight * (1.0 + mod_scale)
    sums = jnp.sum(scaled.reshape(patch, num_dev, feat), axis=2)
    base = jnp.sum(head_weight * mod_shift, axis=1) + head_bias

    mine = lax.dynamic_slice_in_dim(scaled, dev_index * feat, feat, axis=1)
    parts = jnp.einsum("fdt,kd->ftk", hidden, split3(mine), preferred_element_type=F32)
    values = hidden.astype(F32)
    mean = jnp.mean(values, axis=1)
    centred = values - mean[:, None]
    spread = jnp.sum(centred * centred, axis=1)
    part = parts[..., :patch] + (parts[..., patch : 2 * patch] + parts[..., 2 * patch :])
    part = part - mean[..., None] * lax.dynamic_slice_in_dim(sums, dev_index, 1, axis=1)[:, 0]
    part = part.reshape(frames, num_dev, tile, patch).transpose(1, 2, 0, 3).reshape(num_dev, tile, frames * patch)
    stats = jnp.stack([mean, spread]).reshape(2 * frames, num_dev, tile).transpose(1, 0, 2)
    stats = jnp.pad(stats, ((0, 0), (0, 8 - 2 * frames), (0, frames * patch - tile)))
    sent = jnp.concatenate([part, stats], axis=1)
    got = lax.all_to_all(sent, "seq", split_axis=0, concat_axis=0, tiled=True)

    got_part = got[:, :tile].reshape(num_dev, tile, frames, patch)
    got_stat = got[:, tile : tile + 2 * frames, :tile].reshape(num_dev, 2, frames, tile)
    means = got_stat[:, 0]
    total_mean = jnp.mean(means, axis=0)
    off = means - total_mean
    var = (jnp.sum(got_stat[:, 1], axis=0) + feat * jnp.sum(off * off, axis=0)) / (feat * num_dev)
    fixed = jnp.sum(off[..., None] * sums.T[:, None, None, :], axis=0)
    summed = jnp.sum(got_part, axis=0).transpose(1, 0, 2) + fixed
    projected = (summed * lax.rsqrt(var + 1e-06)[..., None] + base).astype(BF16)
    projected = projected.reshape(frames, rows_dev, TOK_W, patch)

    forward = [(i, i + 1) for i in range(num_dev - 1)]
    backward = [(j, i) for i, j in forward]
    low = lax.ppermute(projected[:, -1:], "seq", forward)
    high = lax.ppermute(projected[:, :1], "seq", backward)
    rows = jnp.concatenate([low, projected, high], axis=1)
    latent = rows.reshape(frames, rows_dev + 2, TOK_W, 2, 2 * lat_ch).transpose(0, 1, 3, 2, 4)
    latent = latent.reshape(frames, 2 * rows_dev + 4, TOK_W, 2 * lat_ch)
    left = jnp.pad(latent[:, :, :-1, lat_ch:], ((0, 0), (0, 0), (1, 0), (0, 0)))
    right = jnp.pad(latent[:, :, 1:, :lat_ch], ((0, 0), (0, 0), (0, 1), (0, 0)))
    quad = jnp.concatenate([left, latent, right], axis=-1)
    out_rows = 2 * rows_dev + 2
    x1 = jnp.concatenate([quad[:, b : b + out_rows] for b in range(3)], axis=-1)
    return decode(x1, dev_index, num_dev, conv_in_weight, conv_in_bias, gain_in, up_weight, up_bias, gain_up, out_weight, out_bias)


def solution(mesh):
    placed = (P("grp", "seq", None), P(), P(), P(), P(), P(), P(), P(), P(), P(), P(), P(), P())
    return jax.shard_map(
        local, mesh=mesh, in_specs=placed, out_specs=P("grp", "seq", None, None), check_vma=False
    )
```

time: 138 us -> 63.9 us (0.46)
  the two profiles are of different devices: /device:TPU:13 before, /device:TPU:16 now
where the time goes in v1:
time: 63.9 us; the launch traced here: 63.2 us
  local copies, waits for them, and re-layouts  21.4 us (33%)
  other arithmetic  13.4 us (21%)
  starting transfers between devices  12.8 us (20%)
  Pallas kernels  8.26 us (13%)
  waiting for transfers between devices  6.17 us (10%)
  matrix products  0.68 us (1%)
    pallas_call x1, Pallas kernels, decode(): pl.pallas_call(functools.partial(conv_kernel, num_dev, lat_rows, (c1, c2,...  8.26 us
    all_to_all x1, starting transfers between devices, local(): got = lax.all_to_all(sent, 'seq', split_axis=0, concat_axis=0, tiled=True)  6.18 us
    all_to_all x1, waiting for transfers between devices, local(): got = lax.all_to_all(sent, 'seq', split_axis=0, concat_axis=0, tiled=True)  6.16 us
    ppermute x1, starting transfers between devices, local(): high = lax.ppermute(projected[:, :1], 'seq', backward)  4.72 us
    unnamed x33, local copies, waits for them, and re-layouts  3.28 us
    reshape x1, local copies, waits for them, and re-layouts, decode(): w1 = jnp.stack([jnp.concatenate([taps, none], axis=2), jnp.concatenate([n...  2.76 us
    reduce_sum x1, other arithmetic, local(): base = jnp.sum(head_weight * mod_shift, axis=1) + head_bias  2.64 us
    another operation x2, local copies, waits for them, and re-layouts, decode(): jnp.stack([jnp.concatenate([taps, none], axis=2), jnp.concatenate([none,...  2.54 us
  transfers between devices with their start and end apart: 3, of which 1 were waited for; matrix products, arithmetic and copies ran while one was open for 24% of the time, Pallas kernels for 0%

profile of v1, /device:TPU:16, one launch (start us, length us, event | category | flops | bytes accessed | tf_op | source)
XLA Modules:
  0.0 63.2 jit_solution(14107193131256322988)
XLA Ops:
  0.0 0.7 %broadcast_add_fusion = f32[5120]{0:T(1024)S(1)} fusion(f32[5120]{0:T(1024)} %param.15), kind=kLoop, calls=%fused_computation.63 | loop fusion | flops 5120 | bytes 40960 | tf_op jit(solution)/shard_map/add | solution.py:161
  0.7 2.6 %multiply_reduce_fusion = (f32[64]{0:T(128)S(1)}, f32[64,5120]{1,0:T(8,128)}) fusion(f32[64,5120]{1,0:T(8,128)} %param.16, f32[5120]{0:T(1024)} %param.14, f32[5120]{0:T(1024)S(1)} %broadcast_add_fusion), kind=kLoop, calls=%fused_computation.12 | loop fusion | flops 982976 | bytes 2662656 | tf_op jit(solution)/shard_map/reduce_sum | solution.py:163
  3.4 0.0 copy-start.5
  3.4 1.9 %reshape.79 = f32[64,16,320]{2,1,0:T(8,128)S(1)} reshape(f32[64,5120]{1,0:T(8,128)} %get-tuple-element.18) | data formatting | bytes 2621440 | tf_op jit(solution)/shard_map/reshape | solution.py:162
  5.3 1.0 %reduce-precision_convert_fusion.1 = (bf16[64,320]{1,0:T(8,128)(2,1)S(1)}, bf16[64,320]{1,0:T(8,128)(2,1)S(1)}, bf16[64,320]{1,0:T(8,128)(2,1)S(1)}) fusion(f32[64,5120]{1,0:T(8,128)} %get-tuple-element.18, s32[]{:T(128)S(6)} %select_n.6), kind=kLoop, calls=%fused_computation.51 | loop fusion | flops 143360 | bytes 204804 | tf_op jit(solution)/shard_map/convert_element_type | solution.py:147
  6.3 0.3 convert_reduce_fusion
  6.6 0.5 fusion.1
  7.1 0.2 reduce_sum.84
  7.3 0.0 copy-start.11
  7.3 0.2 dynamic-slice_reduce_fusion
  7.5 0.7 %convolution_bitcast_fusion = f32[2,1280,192]{1,2,0:T(8,128)S(1)} fusion(bf16[2,320,1280]{2,1,0:T(8,128)(2,1)S(1)} %copy-done.5, bf16[64,320]{1,0:T(8,128)(2,1)S(1)} %get-tuple-element.20, bf16[64,320]{1,0:T(8,128)(2,1)S(1)} %get-tuple-element.21, bf16[64,320]{1,0:T(8,128)(2,1)S(1)} %get-tuple-element.19), kind=kOutput, calls=%fused_computation.9 | convolution fusion | flops 314941440 | bytes 3727360 | tf_op jit(solution)/shard_map/fdt,kd->ftk/dot_general | solution.py:166
  8.2 0.1 fusion.5
  8.3 0.6 %reshape.80 = f32[2,16,80,64]{2,1,3,0:T(8,128)S(1)} reshape(f32[2,1280,64]{1,2,0:T(8,128)S(1)} %fusion.5) | data formatting | bytes 1310720 | tf_op jit(solution)/shard_map/reshape | solution.py:173
  8.9 0.3 copy.79
  9.3 0.1 reshape.82
  9.4 0.3 copy.80
  9.7 0.3 select_maximum_fusion
  9.9 0.0 copy-start.6
  10.0 1.2 %copy.81 = f32[16,88,128]{2,1,0:T(8,128)} copy(f32[16,88,128]{1,2,0:T(8,128)S(1)} %select_maximum_fusion) | data formatting | bytes 1441792 | tf_op jit(solution)/shard_map/concatenate | solution.py:176
  11.2 6.2 %all-to-all-start = ((f32[16,88,128]{2,1,0:T(8,128)}), f32[16,88,128]{2,1,0:T(8,128)}, u32[]{:S(2)}, u32[]{:S(2)}) async-start(f32[16,88,128]{2,1,0:T(8,128)} %copy.81), calls=%async_computation | async-start | bytes 1441792 | tf_op jit(solution)/shard_map/all_to_all | solution.py:177
  17.4 0.2 convert_element_type.35
  17.6 0.1 fusion.20
  17.7 0.1 slice_add_fusion.1
  17.9 0.3 maximum_bitcast_fusion
  18.1 0.8 %copy.85 = f32[16,64]{1,0:T(8,128)S(1)} copy(f32[16,64]{0,1:T(8,128)} %bitcast.55) | data formatting | bytes 8192 | tf_op jit(solution)/shard_map/transpose | solution.py:185
  18.9 1.1 %add_convert_fusion.1 = (bf16[2,2,1,384,192]{3,4,2,1,0:T(8,128)(2,1)S(1)}, bf16[2,2,1,384,192]{3,4,2,1,0:T(8,128)(2,1)}) fusion(f32[1,2,3,384,192]{3,4,2,1,0:T(8,128)S(1)} %get-tuple-element.36, f32[1,2,3,384,192]{3,4,2,1,0:T(8,128)S(1)} %get-tuple-element.35), kind=kLoop, calls=%fused_computation.22 | loop fusion | flops 2359296 | bytes 4718592 | tf_op jit(solution)/shard_map/convert.7
  20.0 1.0 %fusion.18 = (bf16[2,2,1,384,192]{3,4,2,1,0:T(8,128)(2,1)S(1)}, bf16[2,2,1,384,192]{3,4,2,1,0:T(8,128)(2,1)}) fusion(f32[1,2,3,384,192]{3,4,2,1,0:T(8,128)S(1)} %get-tuple-element.36, f32[1,2,3,384,192]{3,4,2,1,0:T(8,128)S(1)} %get-tuple-element.35), kind=kLoop, calls=%fused_computation.70 | loop fusion | flops 589824 | bytes 4718592 | tf_op jit(solution)/shard_map/convert.6
  21.0 0.1 pad_maximum_fusion.2
  21.1 0.0 copy-start.10
  21.1 1.6 %copy.88 = bf16[2,2,2,384,192]{4,3,2,1,0:T(8,128)(2,1)} copy(bf16[2,2,2,384,192]{3,4,2,1,0:T(8,128)(2,1)S(1)} %pad_maximum_fusion.2) | data formatting | bytes 2359296 | tf_op jit(solution)/shard_map/stack | solution.py:117
  22.8 0.1 pad_maximum_fusion.3
  22.9 1.6 %copy.89 = bf16[2,2,2,384,192]{4,3,2,1,0:T(8,128)(2,1)} copy(bf16[2,2,2,384,192]{3,4,2,1,0:T(8,128)(2,1)S(1)} %pad_maximum_fusion.3) | data formatting | bytes 2359296 | tf_op jit(solution)/shard_map/stack | solution.py:118
  24.5 0.6 %copy-done.14 = f32[64]{0:T(128)S(1)} copy-done((f32[64]{0:T(128)S(1)}, f32[64]{0:T(128)}, u32[]{:S(2)}) %copy-start.14) | copy-done | bytes 280
  25.1 0.3 slice-done.1
  25.4 0.1 pad_bitcast_fusion.1
  25.5 0.9 %pad_maximum_fusion.5 = bf16[2,3,4,16,2,384]{5,3,2,1,0,4:T(8,128)(2,1)} fusion(bf16[2,3,4,16,1,384]{5,3,2,1,0,4:T(8,128)(2,1)S(1)} %get-tuple-element.30, bf16[2,3,4,16,1,384]{5,3,2,1,0,4:T(8,128)(2,1)S(1)} %get-tuple-element.29), kind=kLoop, calls=%fused_computation.33 | loop fusion | flops 294912 | bytes 1179648 | tf_op jit(solution)/shard_map/stack | solution.py:108
  26.4 0.3 pad_slice_fusion.5
  26.7 1.2 %pad_maximum_fusion.4.w3_ref = bf16[3,768,256]{2,1,0:T(8,128)(2,1)} fusion(bf16[3,768,128]{2,1,0:T(8,128)(2,1)S(1)} %bitcast.54, bf16[3,768,128]{2,1,0:T(8,128)(2,1)S(1)} %bitcast.53), kind=kLoop, calls=%fused_computation.20 | loop fusion | flops 2359296 | bytes 2359296 | tf_op jit(solution)/shard_map/concatenate | solution.py:124
  27.9 0.9 %copy-done.7 = bf16[2,2,2,384,192]{4,3,2,1,0:T(8,128)(2,1)S(1)} copy-done((bf16[2,2,2,384,192]{4,3,2,1,0:T(8,128)(2,1)S(1)}, bf16[2,2,2,384,192]{4,3,2,1,0:T(8,128)(2,1)}, u32[]{:S(2)}) %copy-start.7) | copy-done | bytes 1179672
  28.8 0.6 pad_maximum_fusion.w2_ref
  29.4 6.2 %all-to-all-done = f32[16,88,128]{2,1,0:T(8,128)} async-done(((f32[16,88,128]{2,1,0:T(8,128)}), f32[16,88,128]{2,1,0:T(8,128)}, u32[]{:S(2)}, u32[]{:S(2)}) %all-to-all-start) | async-done | bytes 720928 | tf_op jit(solution)/shard_map/all_to_all | solution.py:177
  35.5 0.8 %slice.106 = f32[16,4,80]{2,1,0:T(4,128)S(1)} slice(f32[16,88,128]{2,1,0:T(8,128)} %all-to-all-done), slice={[0:16], [80:84], [0:80]} | slice | bytes 40960 | tf_op jit(solution)/shard_map/slice | solution.py:180
  36.5 0.0 copy-start.12
  36.5 1.1 %slice_reduce_fusion = f32[80,128]{1,0:T(8,128)S(1)} fusion(f32[16,88,128]{2,1,0:T(8,128)} %all-to-all-done), kind=kLoop, calls=%fused_computation.28 | loop fusion | flops 153600 | bytes 696320 | tf_op jit(solution)/shard_map/reduce_sum | solution.py:186
  37.6 0.1 copy.82
  37.7 0.2 multiply_reduce_fusion.1
  37.9 0.1 fusion.15
  38.0 1.9 %collective-permute-start = (bf16[2,1,80,64]{2,3,0,1:T(8,128)(2,1)S(1)}, bf16[2,1,80,64]{2,3,0,1:T(8,128)(2,1)S(1)}, u32[]{:S(2)}, u32[]{:S(2)}) collective-permute-start(bf16[2,1,80,64]{2,3,0,1:T(8,128)(2,1)S(1)} %fusion.15), channel_id=1, source_target_pairs={{0,1},{1,2},{2,3},{3,4},{4,5},{5,6},{6,7},{7,8},{8,9},{9,10},{10,1... | collective-permute-start | bytes 61448 | tf_op jit(solution)/shard_map/ppermute | solution.py:192
  39.9 4.7 %collective-permute-start.1 = (bf16[2,1,80,64]{2,3,0,1:T(8,128)(2,1)S(1)}, bf16[2,1,80,64]{2,3,0,1:T(8,128)(2,1)S(1)}, u32[]{:S(2)}, u32[]{:S(2)}) collective-permute-start(bf16[2,1,80,64]{2,3,0,1:T(8,128)(2,1)S(1)} %fusion.15), channel_id=1, source_target_pairs={{1,0},{2,1},{3,2},{4,3},{5,4},{6,5},{7,6},{8,7},{9,8},{10,9},{11,1... | collective-permute-start | bytes 61448 | tf_op jit(solution)/shard_map/ppermute | solution.py:193
  44.7 2.5 %copy.87 = bf16[2,3,4,16,2,384]{5,4,3,2,1,0:T(2,128)(2,1)} copy(bf16[2,3,4,16,2,384]{5,3,2,1,0,4:T(8,128)(2,1)} %pad_maximum_fusion.5) | data formatting | bytes 1179648 | tf_op jit(solution)/shard_map/stack | solution.py:108
  47.2 2.8 %reshape.86.w1_ref = bf16[2,192,768]{2,1,0:T(8,128)(2,1)} reshape(bf16[2,3,4,16,2,384]{5,4,3,2,1,0:T(2,128)(2,1)} %copy.87) | data formatting | bytes 1179648 | tf_op jit(solution)/shard_map/reshape | solution.py:110
  50.0 0.1 pad_maximum_fusion.8
  50.1 0.2 copy.86
  50.3 0.2 fusion.22
  50.5 0.0 copy-start.2
  50.5 0.0 copy-start.3
  50.5 0.3 fusion.8
  50.8 0.1 fusion.21
  50.9 0.2 pad_maximum_fusion.6.x_ref
  51.1 0.7 %copy-done = bf16[3,768,256]{2,1,0:T(8,128)(2,1)S(1)} copy-done((bf16[3,768,256]{2,1,0:T(8,128)(2,1)S(1)}, bf16[3,768,256]{2,1,0:T(8,128)(2,1)}, u32[]{:S(2)}) %copy-start) | copy-done | bytes 1179672
  51.7 0.1 copy-done.2
  51.9 8.3 %shard_map.127 = bf16[2560,96]{1,0:T(8,128)(2,1)S(1)} custom-call(s32[1]{0:T(128)} %bitcast.pos_ref, bf16[2,4,80,192]{3,2,1,0:T(8,128)(2,1)S(1)} %pad_maximum_fusion.6.x_ref, bf16[2,192,768]{2,1,0:T(8,128)(2,1)S(1)} %copy-done.2, f32[1,384]{1,0:T(1,128)S(1)} %broadcast_in_dim.13.b1_ref, f32[1,384]{1,0:T(1,128)S(1)} %broadcast_in_dim.14.g1_ref, ...), custom_call_target="tpu_custom_call" | custom-call | tf_op jit(solution)/shard_map/pallas_call | solution.py:128
  60.2 0.8 %copy-done.1 = bf16[2560,96]{1,0:T(8,128)(2,1)} copy-done((bf16[2560,96]{1,0:T(8,128)(2,1)}, bf16[2560,96]{1,0:T(8,128)(2,1)S(1)}, u32[]{:S(2)}) %copy-start.1) | copy-done | bytes 491544
  61.0 2.2 %copy.90 = bf16[2,4,320,96]{2,3,1,0:T(8,128)(2,1)} copy(bf16[2,4,320,96]{3,2,1,0:T(8,128)(2,1)} %bitcast.44) | data formatting | bytes 983040 | tf_op jit(solution)/shard_map/reshape | solution.py:140
  (39 shorter events, 0.2 us)
Async XLA Ops:
  3.4 2.9 %copy-start.5 = (bf16[2,320,1280]{2,1,0:T(8,128)(2,1)S(1)}, bf16[2,320,1280]{2,1,0:T(8,128)(2,1)}, u32[]{:S(2)}) copy-start(bf16[2,320,1280]{2,1,0:T(8,128)(2,1)} %param.13) | copy-start | bytes 4915204
  7.3 0.9 %copy-start.11 = (f32[64,16]{1,0:T(8,128)}, f32[64,16]{1,0:T(8,128)S(1)}, u32[]{:S(2)}) copy-start(f32[64,16]{1,0:T(8,128)S(1)} %reduce_sum.84) | copy-start | bytes 12292
  9.9 7.4 %copy-start.6 = (bf16[3,3,384,192]{2,3,1,0:T(8,128)(2,1)S(1)}, bf16[3,3,384,192]{2,3,1,0:T(8,128)(2,1)}, u32[]{:S(2)}) copy-start(bf16[3,3,384,192]{2,3,1,0:T(8,128)(2,1)} %param.21) | copy-start | bytes 3981316
  11.2 24.4 %all-to-all-start = ((f32[16,88,128]{2,1,0:T(8,128)}), f32[16,88,128]{2,1,0:T(8,128)}, u32[]{:S(2)}, u32[]{:S(2)}) async-start(f32[16,88,128]{2,1,0:T(8,128)} %copy.81), calls=%async_computation | async-start | bytes 1441792 | tf_op jit(solution)/shard_map/all_to_all | solution.py:177
  21.1 1.6 %copy-start.9 = (bf16[2,2,1,384,192]{3,4,2,1,0:T(8,128)(2,1)S(1)}, bf16[2,2,1,384,192]{3,4,2,1,0:T(8,128)(2,1)}, u32[]{:S(2)}) copy-start(bf16[2,2,1,384,192]{3,4,2,1,0:T(8,128)(2,1)} %get-tuple-element.12) | copy-start | bytes 1769476
  21.1 1.6 %copy-start.10 = (bf16[2,2,1,384,192]{3,4,2,1,0:T(8,128)(2,1)S(1)}, bf16[2,2,1,384,192]{3,4,2,1,0:T(8,128)(2,1)}, u32[]{:S(2)}) copy-start(bf16[2,2,1,384,192]{3,4,2,1,0:T(8,128)(2,1)} %get-tuple-element.10) | copy-start | bytes 1769476
  24.5 0.7 %copy-start.14 = (f32[64]{0:T(128)S(1)}, f32[64]{0:T(128)}, u32[]{:S(2)}) copy-start(f32[64]{0:T(128)} %param.17) | copy-start | bytes 772
  24.5 0.9 %slice-start.1 = ((bf16[3,3,3,16,384]{4,3,2,1,0:T(8,128)(2,1)}), bf16[2,3,3,16,384]{4,3,2,1,0:T(8,128)(2,1)S(1)}, s32[]{:S(2)}) async-start(bf16[3,3,3,16,384]{4,3,2,1,0:T(8,128)(2,1)} %param.18), calls=%async_computation.2 | async-start | bytes 442368 | tf_op jit(solution)/shard_map/slice | solution.py:106
  24.5 1.9 %slice-start = ((bf16[3,3,3,192,96]{4,3,2,1,0:T(8,128)(2,1)}), bf16[2,3,3,192,96]{4,3,2,1,0:T(8,128)(2,1)S(1)}, s32[]{:S(2)}) async-start(bf16[3,3,3,192,96]{4,3,2,1,0:T(8,128)(2,1)} %param.24), calls=%async_computation.1 | async-start | bytes 1769472 | tf_op jit(solution)/shard_map/slice | solution.py:123
  26.4 1.5 %copy-start.8 = (bf16[2,2,2,384,192]{4,3,2,1,0:T(8,128)(2,1)S(1)}, bf16[2,2,2,384,192]{4,3,2,1,0:T(8,128)(2,1)}, u32[]{:S(2)}) copy-start(bf16[2,2,2,384,192]{4,3,2,1,0:T(8,128)(2,1)} %copy.89) | copy-start | bytes 3538948
  26.7 2.1 %copy-start.7 = (bf16[2,2,2,384,192]{4,3,2,1,0:T(8,128)(2,1)S(1)}, bf16[2,2,2,384,192]{4,3,2,1,0:T(8,128)(2,1)}, u32[]{:S(2)}) copy-start(bf16[2,2,2,384,192]{4,3,2,1,0:T(8,128)(2,1)} %copy.88) | copy-start | bytes 3538948
  28.8 15.9 %copy-start.15 = (f32[96]{0:T(128)S(1)}, f32[96]{0:T(128)}, u32[]{:S(2)}) copy-start(f32[96]{0:T(128)} %param.25) | copy-start | bytes 1156
  36.5 13.5 %copy-start.12 = (f32[384]{0:T(512)S(1)}, f32[384]{0:T(512)}, u32[]{:S(2)}) copy-start(f32[384]{0:T(512)} %param.19) | copy-start | bytes 4612
  36.5 13.5 %copy-start.13 = (f32[384]{0:T(512)S(1)}, f32[384]{0:T(512)}, u32[]{:S(2)}) copy-start(f32[384]{0:T(512)} %param.20) | copy-start | bytes 4612
  38.0 11.9 %collective-permute-start = (bf16[2,1,80,64]{2,3,0,1:T(8,128)(2,1)S(1)}, bf16[2,1,80,64]{2,3,0,1:T(8,128)(2,1)S(1)}, u32[]{:S(2)}, u32[]{:S(2)}) collective-permute-start(bf16[2,1,80,64]{2,3,0,1:T(8,128)(2,1)S(1)} %fusion.15), channel_id=1, source_target_pairs={{0,1},{1,2},{2,3},{3,4},{4,5},{5,6},{6,7},{7,8},{8,9},{9,10},{10,1... | collective-permute-start | bytes 61448 | tf_op jit(solution)/shard_map/ppermute | solution.py:192
  39.9 10.0 %collective-permute-start.1 = (bf16[2,1,80,64]{2,3,0,1:T(8,128)(2,1)S(1)}, bf16[2,1,80,64]{2,3,0,1:T(8,128)(2,1)S(1)}, u32[]{:S(2)}, u32[]{:S(2)}) collective-permute-start(bf16[2,1,80,64]{2,3,0,1:T(8,128)(2,1)S(1)} %fusion.15), channel_id=1, source_target_pairs={{1,0},{2,1},{3,2},{4,3},{5,4},{6,5},{7,6},{8,7},{9,8},{10,9},{11,1... | collective-permute-start | bytes 61448 | tf_op jit(solution)/shard_map/ppermute | solution.py:193
  50.5 1.3 %copy-start = (bf16[3,768,256]{2,1,0:T(8,128)(2,1)S(1)}, bf16[3,768,256]{2,1,0:T(8,128)(2,1)}, u32[]{:S(2)}) copy-start(bf16[3,768,256]{2,1,0:T(8,128)(2,1)} %pad_maximum_fusion.4.w3_ref) | copy-start | bytes 3538948
  50.5 1.4 %copy-start.2 = (bf16[2,192,768]{2,1,0:T(8,128)(2,1)S(1)}, bf16[2,192,768]{2,1,0:T(8,128)(2,1)}, u32[]{:S(2)}) copy-start(bf16[2,192,768]{2,1,0:T(8,128)(2,1)} %reshape.86.w1_ref) | copy-start | bytes 1769476
  50.5 1.4 %copy-start.3 = (f32[192]{0:T(256)S(1)}, f32[192]{0:T(256)}, u32[]{:S(2)}) copy-start(f32[192]{0:T(256)} %param.22) | copy-start | bytes 2308
  50.5 1.4 %copy-start.4 = (f32[192]{0:T(256)S(1)}, f32[192]{0:T(256)}, u32[]{:S(2)}) copy-start(f32[192]{0:T(256)} %param.23) | copy-start | bytes 2308
  60.2 0.8 %copy-start.1 = (bf16[2560,96]{1,0:T(8,128)(2,1)}, bf16[2560,96]{1,0:T(8,128)(2,1)S(1)}, u32[]{:S(2)}) copy-start(bf16[2560,96]{1,0:T(8,128)(2,1)S(1)} %shard_map.127) | copy-start | bytes 1474564

commit v2 on v1

--- a/solution.py
+++ b/solution.py
@@ -28,8 +28,16 @@
 
 
 def conv_kernel(num_dev, lat_rows, chans, pos_ref, x_ref, w1_ref, b1_ref, g1_ref, w2_ref, b2_ref, g2_ref,
-                w3_ref, b3_ref, out_ref, act1, act2, res):
+                w3_ref, b3_ref, out_ref, act1, act2, res, w1s):
     c1, c2, c3 = chans
+    ch = w1_ref.shape[3]
+    blank = jnp.zeros((ch, c1), BF16)
+    for a in range(2):
+        for b in range(3):
+            for j in range(4):
+                rows = slice((4 * b + j) * ch, (4 * b + j + 1) * ch)
+                w1s[a, rows, 0:c1] = w1_ref[a + 1, b, j] if j < 3 else blank
+                w1s[a, rows, c1 : 2 * c1] = w1_ref[a + 1, b, j - 1] if j > 0 else blank
     dev = pos_ref[0]
     rows1 = lat_rows + 2
     m1 = rows1 * TOK_W
@@ -45,10 +53,10 @@
     keep1 = inside(m1, dev * lat_rows - 1, 1, num_dev * lat_rows)
     for frame in range(2):
         x_now = x_ref[frame].reshape(m1, x_ref.shape[-1])
-        pre = jnp.dot(x_now, w1_ref[1], preferred_element_type=F32)
+        pre = jnp.dot(x_now, w1s[1], preferred_element_type=F32)
         if frame == 1:
             x_old = x_ref[0].reshape(m1, x_ref.shape[-1])
-            pre = pre + jnp.dot(x_old, w1_ref[0], preferred_element_type=F32)
+            pre = pre + jnp.dot(x_old, w1s[0], preferred_element_type=F32)
         for r in range(2):
             val = rms_silu(pre[:, r * c1 : (r + 1) * c1] + b1_ref[...], g1_ref[...])
             val = jnp.where(keep1, val, 0.0)
@@ -95,7 +103,9 @@
             new = two if new is None else new + two
         res[pl.ds(s, m3, stride=4), :] = old[:, 0:128] + b3_ref[...]
         res[pl.ds(4 * m3 + s, m3, stride=4), :] = old[:, 128:256] + new + b3_ref[...]
-    out_ref[...] = res[:, 0:c3].astype(BF16)
+    width = 4 * TOK_W
+    for i in range(2 * rows3):
+        out_ref[i] = jnp.transpose(res[i * width : (i + 1) * width, :])[0:c3].astype(BF16)
 
 
 def decode(x1, dev_index, num_dev, conv_in_weight, conv_in_bias, gain_in, up_weight, up_bias, gain_up, out_weight, out_bias):
@@ -103,11 +113,6 @@
     lat_rows = rows1 - 2
     lat_ch, c1 = conv_in_weight.shape[3:]
     c2, c3 = out_weight.shape[3:]
-    taps = conv_in_weight[1:]
-    none = jnp.zeros_like(taps[:, :, :1])
-    w1 = jnp.stack(
-        [jnp.concatenate([taps, none], axis=2), jnp.concatenate([none, taps], axis=2)], axis=4
-    ).reshape(2, 12 * lat_ch, 2 * c1)
     wide = up_weight.astype(F32)
     by_row = jnp.stack(
         [jnp.stack([wide[0], wide[1] + wide[2]]), jnp.stack([wide[0] + wide[1], wide[2]])]
@@ -127,17 +132,18 @@
     vmem = pl.BlockSpec(memory_space=pltpu.VMEM)
     out = pl.pallas_call(
         functools.partial(conv_kernel, num_dev, lat_rows, (c1, c2, c3)),
-        out_shape=jax.ShapeDtypeStruct((cells, c3), BF16),
+        out_shape=jax.ShapeDtypeStruct((frames * 2 * lat_rows, c3, 4 * cols), BF16),
         in_specs=[pl.BlockSpec(memory_space=pltpu.SMEM)] + [vmem] * 9,
         out_specs=vmem,
         scratch_shapes=[
             pltpu.VMEM((frames, rows1, cols, 4 * c1), BF16),
             pltpu.VMEM((frames, 2 * lat_rows + 2, cols, 6 * 256), BF16),
             pltpu.VMEM((cells, 128), F32),
+            pltpu.VMEM((2, 12 * lat_ch, 2 * c1), BF16),
         ],
         compiler_params=pltpu.CompilerParams(vmem_limit_bytes=40 * 1024 * 1024),
-    )(dev_index[None].astype(jnp.int32), x1, w1, conv_in_bias[None], gain_in[None], w2, up_bias[None], gain_up[None], w3, b3)
-    return out.reshape(frames, 2 * lat_rows, 4 * cols, c3)
+    )(dev_index[None].astype(jnp.int32), x1, conv_in_weight, conv_in_bias[None], gain_in[None], w2, up_bias[None], gain_up[None], w3, b3)
+    return out.reshape(frames, 2 * lat_rows, c3, 4 * cols).transpose(0, 1, 3, 2)
 
 
 def split3(weight):
@@ -169,7 +175,7 @@
     centred = values - mean[:, None]
     spread = jnp.sum(centred * centred, axis=1)
     part = parts[..., :patch] + (parts[..., patch : 2 * patch] + parts[..., 2 * patch :])
-    part = part - mean[..., None] * lax.dynamic_slice_in_dim(sums, dev_index, 1, axis=1)[:, 0]
+    part = part - mean[..., None] * jnp.sum(mine, axis=1)
     part = part.reshape(frames, num_dev, tile, patch).transpose(1, 2, 0, 3).reshape(num_dev, tile, frames * patch)
     stats = jnp.stack([mean, spread]).reshape(2 * frames, num_dev, tile).transpose(1, 0, 2)
     stats = jnp.pad(stats, ((0, 0), (0, 8 - 2 * frames), (0, frames * patch - tile)))

time: 63.9 us -> 63.4 us (level)
  the two profiles are of different devices: /device:TPU:16 before, /device:TPU:13 now
where the time goes in v2:
time: 63.4 us; the launch traced here: 62.8 us
  local copies, waits for them, and re-layouts  17.4 us (27%)
  other arithmetic  15.6 us (25%)
  starting transfers between devices  12.2 us (19%)
  Pallas kernels  9.31 us (15%)
  waiting for transfers between devices  7.27 us (11%)
  matrix products  0.68 us (1%)
    pallas_call x1, Pallas kernels, decode(): pl.pallas_call(functools.partial(conv_kernel, num_dev, lat_rows, (c1, c2,...  9.31 us
    all_to_all x1, starting transfers between devices, local(): got = lax.all_to_all(sent, 'seq', split_axis=0, concat_axis=0, tiled=True)  6.52 us
    ppermute x1, waiting for transfers between devices, local(): high = lax.ppermute(projected[:, :1], 'seq', backward)  3.95 us
    ppermute x1, starting transfers between devices, local(): low = lax.ppermute(projected[:, -1:], 'seq', forward)  3.61 us
    all_to_all x1, waiting for transfers between devices, local(): got = lax.all_to_all(sent, 'seq', split_axis=0, concat_axis=0, tiled=True)  3.31 us
    unnamed x29, local copies, waits for them, and re-layouts  3.24 us
    reshape x2, local copies, waits for them, and re-layouts, local(): part.reshape(frames, num_dev, tile, patch).transpose(1, 2, 0, 3)  3.17 us
    concatenate x1, local copies, waits for them, and re-layouts, local(): sent = jnp.concatenate([part, stats], axis=1)  2.53 us
  transfers between devices with their start and end apart: 3, of which 2 were waited for; matrix products, arithmetic and copies ran while one was open for 18% of the time, Pallas kernels for 0%

profile of v2, /device:TPU:13, one launch (start us, length us, event | category | flops | bytes accessed | tf_op | source)
XLA Modules:
  0.0 62.8 jit_solution(2578726660304197916)
XLA Ops:
  0.0 0.9 %broadcast_add_fusion = f32[5120]{0:T(1024)S(1)} fusion(f32[5120]{0:T(1024)} %param.15), kind=kLoop, calls=%fused_computation.60 | loop fusion | flops 5120 | bytes 40960 | tf_op jit(solution)/shard_map/add | solution.py:167
  0.9 1.7 %convert_reduce_fusion = f32[2,1280]{1,0:T(2,128)S(1)} fusion(bf16[2,320,1280]{2,1,0:T(8,128)(2,1)} %param.13), kind=kLoop, calls=%fused_computation.5 | loop fusion | flops 1635840 | bytes 1648640 | tf_op jit(solution)/shard_map/reduce_sum | solution.py:174
  2.6 0.0 copy-done.4
  2.6 0.5 fusion.1
  3.1 0.0 copy-done.9
  3.1 1.6 %multiply_reduce_fusion = (f32[64]{0:T(128)S(1)}, f32[64,5120]{1,0:T(8,128)S(1)}) fusion(f32[64,5120]{1,0:T(8,128)} %param.16, f32[5120]{0:T(1024)S(1)} %copy-done.9, f32[5120]{0:T(1024)S(1)} %broadcast_add_fusion), kind=kLoop, calls=%fused_computation.12 | loop fusion | flops 982976 | bytes 2662656 | tf_op jit(solution)/shard_map/reduce_sum | solution.py:169
  4.7 0.2 dynamic-slice_reduce_fusion
  4.9 0.7 %convolution_bitcast_fusion = f32[2,1280,192]{1,2,0:T(8,128)S(1)} fusion(bf16[2,320,1280]{2,1,0:T(8,128)(2,1)S(1)} %copy-done.4, bf16[64,320]{1,0:T(8,128)(2,1)S(1)} %get-tuple-element.21, bf16[64,320]{1,0:T(8,128)(2,1)S(1)} %get-tuple-element.20, bf16[64,320]{1,0:T(8,128)(2,1)S(1)} %get-tuple-element.22), kind=kOutput, calls=%fused_computation.9 | convolution fusion | flops 314941440 | bytes 3727360 | tf_op jit(solution)/shard_map/fdt,kd->ftk/dot_general | solution.py:172
  5.5 0.1 fusion.5
  5.7 1.6 %reshape.76 = f32[2,16,80,64]{2,1,3,0:T(8,128)} reshape(f32[2,1280,64]{1,2,0:T(8,128)S(1)} %fusion.5) | data formatting | bytes 1310720 | tf_op jit(solution)/shard_map/reshape | solution.py:179
  7.3 1.6 %copy.56 = f32[2,16,80,64]{2,3,0,1:T(8,128)S(1)} copy(f32[2,16,80,64]{2,1,3,0:T(8,128)} %reshape.76) | data formatting | bytes 1310720 | tf_op jit(solution)/shard_map/reshape | solution.py:179
  8.9 0.1 reshape.78
  9.0 1.2 %copy.57 = f32[4,16,80]{0,2,1:T(8,128)} copy(f32[4,16,80]{2,1,0:T(8,128)S(1)} %reshape.78) | data formatting | bytes 40960 | tf_op jit(solution)/shard_map/reshape | solution.py:180
  10.1 2.3 %select_maximum_fusion = f32[16,88,128]{1,2,0:T(8,128)} fusion(f32[16,4,80]{1,2,0:T(8,128)} %bitcast.49, f32[16,80,128]{1,2,0:T(8,128)S(1)} %bitcast.46), kind=kLoop, calls=%fused_computation.23 | loop fusion | flops 540672 | bytes 1396736 | tf_op jit(solution)/shard_map/concatenate | solution.py:182
  12.4 2.5 %copy.58 = f32[16,88,128]{2,1,0:T(8,128)} copy(f32[16,88,128]{1,2,0:T(8,128)} %select_maximum_fusion) | data formatting | bytes 1441792 | tf_op jit(solution)/shard_map/concatenate | solution.py:182
  15.0 6.5 %all-to-all-start = ((f32[16,88,128]{2,1,0:T(8,128)}), f32[16,88,128]{2,1,0:T(8,128)}, u32[]{:S(2)}, u32[]{:S(2)}) async-start(f32[16,88,128]{2,1,0:T(8,128)} %copy.58), calls=%async_computation | async-start | bytes 1441792 | tf_op jit(solution)/shard_map/all_to_all | solution.py:183
  21.5 0.0 copy-done.5
  21.5 0.2 convert_element_type.35
  21.7 1.4 %slice_add_fusion.1 = (f32[1,3,384,192]{2,3,1,0:T(8,128)}, f32[1,3,384,192]{2,3,1,0:T(8,128)}) fusion(f32[3,3,384,192]{2,3,1,0:T(8,128)S(1)} %convert_element_type.35), kind=kLoop, calls=%fused_computation.27 | loop fusion | flops 442368 | bytes 4423680 | tf_op jit(solution)/shard_map/add | solution.py:118
  23.1 1.3 %fusion.20 = (f32[1,3,384,192]{2,3,1,0:T(8,128)}, f32[1,3,384,192]{2,3,1,0:T(8,128)}) fusion(bf16[3,3,384,192]{2,3,1,0:T(8,128)(2,1)S(1)} %copy-done.5), kind=kLoop, calls=%fused_computation.69 | loop fusion | bytes 3538944 | tf_op jit(solution)/shard_map/slice | solution.py:118
  24.4 0.5 reshape.80
  24.9 0.0 copy-start.8
  24.9 0.2 reduce_sum.98
  25.1 0.1 copy.62
  25.2 0.9 %copy-done.8 = f32[1,3,384,192]{2,3,1,0:T(8,128)S(1)} copy-done((f32[1,3,384,192]{2,3,1,0:T(8,128)S(1)}, f32[1,3,384,192]{2,3,1,0:T(8,128)}, u32[]{:S(2)}) %copy-start.8) | copy-done | bytes 884760
  26.1 1.9 %maximum_bitcast_fusion = (f32[1,2,3,384,192]{3,4,2,1,0:T(8,128)S(1)}, f32[1,2,3,384,192]{3,4,2,1,0:T(8,128)S(1)}) fusion(f32[1,3,384,192]{2,3,1,0:T(8,128)} %get-tuple-element.13, f32[1,3,384,192]{2,3,1,0:T(8,128)S(1)} %copy-done.8, f32[1,3,384,192]{2,3,1,0:T(8,128)} %get-tuple-element.16, f32[1,3,384,192]{2,3,1,0:T(8,128)} %get-tuple-element.14), kind=kLoop, calls=%fused_computation.10 | loop fusion | flops 884736 | bytes 7077888 | tf_op jit(solution)/shard_map/stack | solution.py:117
  28.0 0.3 add_convert_fusion.1
  28.3 0.2 fusion.18
  28.5 0.1 pad_maximum_fusion.2
  28.6 1.6 %copy.64 = bf16[2,2,2,384,192]{4,3,2,1,0:T(8,128)(2,1)} copy(bf16[2,2,2,384,192]{3,4,2,1,0:T(8,128)(2,1)S(1)} %pad_maximum_fusion.2) | data formatting | bytes 2359296 | tf_op jit(solution)/shard_map/stack | solution.py:122
  30.2 0.1 pad_maximum_fusion.3
  30.4 1.6 %copy.65 = bf16[2,2,2,384,192]{4,3,2,1,0:T(8,128)(2,1)} copy(bf16[2,2,2,384,192]{3,4,2,1,0:T(8,128)(2,1)S(1)} %pad_maximum_fusion.3) | data formatting | bytes 2359296 | tf_op jit(solution)/shard_map/stack | solution.py:123
  31.9 0.7 %copy-done.12 = f32[64]{0:T(128)S(1)} copy-done((f32[64]{0:T(128)S(1)}, f32[64]{0:T(128)}, u32[]{:S(2)}) %copy-start.12) | copy-done | bytes 280
  32.6 0.5 slice-done
  33.1 0.3 pad_slice_fusion.5
  33.4 1.2 %pad_maximum_fusion.4.w3_ref = bf16[3,768,256]{2,1,0:T(8,128)(2,1)} fusion(bf16[3,768,128]{2,1,0:T(8,128)(2,1)S(1)} %bitcast.51, bf16[3,768,128]{2,1,0:T(8,128)(2,1)S(1)} %bitcast.50), kind=kLoop, calls=%fused_computation.20 | loop fusion | flops 2359296 | bytes 2359296 | tf_op jit(solution)/shard_map/concatenate | solution.py:129
  34.6 0.0 copy-done.7
  34.6 0.9 %copy-done.6 = bf16[2,2,2,384,192]{4,3,2,1,0:T(8,128)(2,1)S(1)} copy-done((bf16[2,2,2,384,192]{4,3,2,1,0:T(8,128)(2,1)S(1)}, bf16[2,2,2,384,192]{4,3,2,1,0:T(8,128)(2,1)}, u32[]{:S(2)}) %copy-start.6) | copy-done | bytes 1179672
  35.5 0.6 pad_maximum_fusion.w2_ref
  36.1 3.3 %all-to-all-done = f32[16,88,128]{2,1,0:T(8,128)} async-done(((f32[16,88,128]{2,1,0:T(8,128)}), f32[16,88,128]{2,1,0:T(8,128)}, u32[]{:S(2)}, u32[]{:S(2)}) %all-to-all-start) | async-done | bytes 720928 | tf_op jit(solution)/shard_map/all_to_all | solution.py:183
  39.4 0.8 %slice.102 = f32[16,4,80]{2,1,0:T(4,128)S(1)} slice(f32[16,88,128]{2,1,0:T(8,128)} %all-to-all-done), slice={[0:16], [80:84], [0:80]} | slice | bytes 40960 | tf_op jit(solution)/shard_map/slice | solution.py:186
  40.3 1.1 %slice_reduce_fusion = f32[80,128]{1,0:T(8,128)S(1)} fusion(f32[16,88,128]{2,1,0:T(8,128)} %all-to-all-done), kind=kLoop, calls=%fused_computation.28 | loop fusion | flops 153600 | bytes 696320 | tf_op jit(solution)/shard_map/reduce_sum | solution.py:192
  41.5 0.1 copy.59
  41.6 0.2 multiply_reduce_fusion.1
  41.8 0.1 fusion.15
  41.9 3.6 %collective-permute-start = (bf16[2,1,80,64]{2,3,0,1:T(8,128)(2,1)S(1)}, bf16[2,1,80,64]{2,3,0,1:T(8,128)(2,1)S(1)}, u32[]{:S(2)}, u32[]{:S(2)}) collective-permute-start(bf16[2,1,80,64]{2,3,0,1:T(8,128)(2,1)S(1)} %fusion.15), channel_id=1, source_target_pairs={{0,1},{1,2},{2,3},{3,4},{4,5},{5,6},{6,7},{7,8},{8,9},{9,10},{10,1... | collective-permute-start | bytes 61448 | tf_op jit(solution)/shard_map/ppermute | solution.py:198
  45.5 2.1 %collective-permute-start.1 = (bf16[2,1,80,64]{2,3,0,1:T(8,128)(2,1)S(1)}, bf16[2,1,80,64]{2,3,0,1:T(8,128)(2,1)S(1)}, u32[]{:S(2)}, u32[]{:S(2)}) collective-permute-start(bf16[2,1,80,64]{2,3,0,1:T(8,128)(2,1)S(1)} %fusion.15), channel_id=1, source_target_pairs={{1,0},{2,1},{3,2},{4,3},{5,4},{6,5},{7,6},{8,7},{9,8},{10,9},{11,1... | collective-permute-start | bytes 61448 | tf_op jit(solution)/shard_map/ppermute | solution.py:199
  47.6 0.0 copy-done.13
  47.6 0.0 copy-done.10
  47.7 0.0 collective-permute-done
  47.7 3.9 %collective-permute-done.1 = bf16[2,1,80,64]{2,3,0,1:T(8,128)(2,1)S(1)} collective-permute-done((bf16[2,1,80,64]{2,3,0,1:T(8,128)(2,1)S(1)}, bf16[2,1,80,64]{2,3,0,1:T(8,128)(2,1)S(1)}, u32[]{:S(2)}, u32[]{:S(2)}) %collective-permute-start.1) | collective-permute-done | bytes 20512 | tf_op jit(solution)/shard_map/ppermute | solution.py:199
  51.7 0.1 pad_maximum_fusion.7
  51.8 0.2 copy.63
  52.0 0.2 fusion.22
  52.1 0.0 copy-start.1
  52.1 0.0 copy-start.2
  52.2 0.0 copy-start.3
  52.2 0.3 fusion.8
  52.5 0.1 fusion.21
  52.5 0.2 pad_maximum_fusion.5.x_ref
  52.7 0.7 %copy-done = bf16[3,768,256]{2,1,0:T(8,128)(2,1)S(1)} copy-done((bf16[3,768,256]{2,1,0:T(8,128)(2,1)S(1)}, bf16[3,768,256]{2,1,0:T(8,128)(2,1)}, u32[]{:S(2)}) %copy-start) | copy-done | bytes 1179672
  53.4 0.1 copy-done.1
  53.5 0.0 copy-done.3
  53.5 9.3 %shard_map.127 = bf16[8,96,320]{2,1,0:T(8,128)(2,1)} custom-call(s32[1]{0:T(128)} %bitcast.pos_ref, bf16[2,4,80,192]{3,2,1,0:T(8,128)(2,1)S(1)} %pad_maximum_fusion.5.x_ref, bf16[3,3,3,16,384]{4,3,2,1,0:T(8,128)(2,1)S(1)} %copy-done.1, f32[1,384]{1,0:T(1,128)S(1)} %broadcast_in_dim.13.b1_ref, f32[1,384]{1,0:T(1,128)S(1)} %broadcast_in_dim.14.g1_ref, ...), custom_call_target="tpu_custom_call" | custom-call | tf_op jit(solution)/shard_map/pallas_call | solution.py:133
  (27 shorter events, 0.2 us)
Async XLA Ops:
  0.0 2.6 %copy-start.4 = (bf16[2,320,1280]{2,1,0:T(8,128)(2,1)S(1)}, bf16[2,320,1280]{2,1,0:T(8,128)(2,1)}, u32[]{:S(2)}) copy-start(bf16[2,320,1280]{2,1,0:T(8,128)(2,1)} %param.13) | copy-start | bytes 4915204
  0.9 2.2 %copy-start.9 = (f32[5120]{0:T(1024)S(1)}, f32[5120]{0:T(1024)}, u32[]{:S(2)}) copy-start(f32[5120]{0:T(1024)} %param.14) | copy-start | bytes 61444
  12.4 9.1 %copy-start.5 = (bf16[3,3,384,192]{2,3,1,0:T(8,128)(2,1)S(1)}, bf16[3,3,384,192]{2,3,1,0:T(8,128)(2,1)}, u32[]{:S(2)}) copy-start(bf16[3,3,384,192]{2,3,1,0:T(8,128)(2,1)} %param.21) | copy-start | bytes 3981316
  15.0 24.5 %all-to-all-start = ((f32[16,88,128]{2,1,0:T(8,128)}), f32[16,88,128]{2,1,0:T(8,128)}, u32[]{:S(2)}, u32[]{:S(2)}) async-start(f32[16,88,128]{2,1,0:T(8,128)} %copy.58), calls=%async_computation | async-start | bytes 1441792 | tf_op jit(solution)/shard_map/all_to_all | solution.py:183
  24.9 1.2 %copy-start.8 = (f32[1,3,384,192]{2,3,1,0:T(8,128)S(1)}, f32[1,3,384,192]{2,3,1,0:T(8,128)}, u32[]{:S(2)}) copy-start(f32[1,3,384,192]{2,3,1,0:T(8,128)} %get-tuple-element.15) | copy-start | bytes 2654212
  31.9 0.7 %copy-start.12 = (f32[64]{0:T(128)S(1)}, f32[64]{0:T(128)}, u32[]{:S(2)}) copy-start(f32[64]{0:T(128)} %param.17) | copy-start | bytes 772
  31.9 1.2 %slice-start = ((bf16[3,3,3,192,96]{4,3,2,1,0:T(8,128)(2,1)}), bf16[2,3,3,192,96]{4,3,2,1,0:T(8,128)(2,1)S(1)}, s32[]{:S(2)}) async-start(bf16[3,3,3,192,96]{4,3,2,1,0:T(8,128)(2,1)} %param.24), calls=%async_computation.1 | async-start | bytes 1769472 | tf_op jit(solution)/shard_map/slice | solution.py:128
  33.1 1.5 %copy-start.7 = (bf16[2,2,2,384,192]{4,3,2,1,0:T(8,128)(2,1)S(1)}, bf16[2,2,2,384,192]{4,3,2,1,0:T(8,128)(2,1)}, u32[]{:S(2)}) copy-start(bf16[2,2,2,384,192]{4,3,2,1,0:T(8,128)(2,1)} %copy.65) | copy-start | bytes 3538948
  33.4 2.1 %copy-start.6 = (bf16[2,2,2,384,192]{4,3,2,1,0:T(8,128)(2,1)S(1)}, bf16[2,2,2,384,192]{4,3,2,1,0:T(8,128)(2,1)}, u32[]{:S(2)}) copy-start(bf16[2,2,2,384,192]{4,3,2,1,0:T(8,128)(2,1)} %copy.64) | copy-start | bytes 3538948
  35.5 12.1 %copy-start.13 = (f32[96]{0:T(128)S(1)}, f32[96]{0:T(128)}, u32[]{:S(2)}) copy-start(f32[96]{0:T(128)} %param.25) | copy-start | bytes 1156
  35.5 12.1 %copy-start.10 = (f32[384]{0:T(512)S(1)}, f32[384]{0:T(512)}, u32[]{:S(2)}) copy-start(f32[384]{0:T(512)} %param.19) | copy-start | bytes 4612
  35.5 12.1 %copy-start.11 = (f32[384]{0:T(512)S(1)}, f32[384]{0:T(512)}, u32[]{:S(2)}) copy-start(f32[384]{0:T(512)} %param.20) | copy-start | bytes 4612
  41.9 5.8 %collective-permute-start = (bf16[2,1,80,64]{2,3,0,1:T(8,128)(2,1)S(1)}, bf16[2,1,80,64]{2,3,0,1:T(8,128)(2,1)S(1)}, u32[]{:S(2)}, u32[]{:S(2)}) collective-permute-start(bf16[2,1,80,64]{2,3,0,1:T(8,128)(2,1)S(1)} %fusion.15), channel_id=1, source_target_pairs={{0,1},{1,2},{2,3},{3,4},{4,5},{5,6},{6,7},{7,8},{8,9},{9,10},{10,1... | collective-permute-start | bytes 61448 | tf_op jit(solution)/shard_map/ppermute | solution.py:198
  45.5 6.1 %collective-permute-start.1 = (bf16[2,1,80,64]{2,3,0,1:T(8,128)(2,1)S(1)}, bf16[2,1,80,64]{2,3,0,1:T(8,128)(2,1)S(1)}, u32[]{:S(2)}, u32[]{:S(2)}) collective-permute-start(bf16[2,1,80,64]{2,3,0,1:T(8,128)(2,1)S(1)} %fusion.15), channel_id=1, source_target_pairs={{1,0},{2,1},{3,2},{4,3},{5,4},{6,5},{7,6},{8,7},{9,8},{10,9},{11,1... | collective-permute-start | bytes 61448 | tf_op jit(solution)/shard_map/ppermute | solution.py:199
  52.1 1.3 %copy-start = (bf16[3,768,256]{2,1,0:T(8,128)(2,1)S(1)}, bf16[3,768,256]{2,1,0:T(8,128)(2,1)}, u32[]{:S(2)}) copy-start(bf16[3,768,256]{2,1,0:T(8,128)(2,1)} %pad_maximum_fusion.4.w3_ref) | copy-start | bytes 3538948
  52.1 1.3 %copy-start.1 = (bf16[3,3,3,16,384]{4,3,2,1,0:T(8,128)(2,1)S(1)}, bf16[3,3,3,16,384]{4,3,2,1,0:T(8,128)(2,1)}, u32[]{:S(2)}) copy-start(bf16[3,3,3,16,384]{4,3,2,1,0:T(8,128)(2,1)} %w1_ref.1) | copy-start | bytes 995332
  52.1 1.3 %copy-start.2 = (f32[192]{0:T(256)S(1)}, f32[192]{0:T(256)}, u32[]{:S(2)}) copy-start(f32[192]{0:T(256)} %param.22) | copy-start | bytes 2308
  52.2 1.3 %copy-start.3 = (f32[192]{0:T(256)S(1)}, f32[192]{0:T(256)}, u32[]{:S(2)}) copy-start(f32[192]{0:T(256)} %param.23) | copy-start | bytes 2308

commit v3 on v2

--- a/solution.py
+++ b/solution.py
@@ -146,11 +146,33 @@
     return out.reshape(frames, 2 * lat_rows, c3, 4 * cols).transpose(0, 1, 3, 2)
 
 
-def split3(weight):
-    high = lax.reduce_precision(weight, 8, 7)
-    rest = weight - high
-    mid = lax.reduce_precision(rest, 8, 7)
-    return jnp.concatenate([high.astype(BF16), mid.astype(BF16), (rest - mid).astype(BF16)], axis=0)
+def head_kernel(num_dev, x_ref, w_ref, out_ref):
+    frames, feat, total = x_ref.shape
+    tile = total // num_dev
+    weight = w_ref[...]
+    patch = weight.shape[0]
+    high = weight.astype(BF16)
+    rest = weight - high.astype(F32)
+    mid = rest.astype(BF16)
+    low = (rest - mid.astype(F32)).astype(BF16)
+    stack = jnp.concatenate([high, mid, low], axis=0)
+    sums = jnp.sum(weight, axis=1, keepdims=True)
+    parts, means, spreads = [], [], []
+    for f in range(frames):
+        full = jnp.dot(stack, x_ref[f], preferred_element_type=F32)
+        values = x_ref[f].astype(F32)
+        mean = jnp.sum(values, axis=0, keepdims=True) * (1.0 / feat)
+        centred = values - mean
+        means.append(mean)
+        spreads.append(jnp.sum(centred * centred, axis=0, keepdims=True))
+        part = full[:patch] + (full[patch : 2 * patch] + full[2 * patch :])
+        parts.append(part - sums * mean)
+    both = jnp.concatenate(parts, axis=0)
+    out_ref[:, 0:tile, :] = jnp.transpose(both).reshape(num_dev, tile, frames * patch)
+    out_ref[:, tile : tile + 8, :] = jnp.zeros((num_dev, 8, frames * patch), F32)
+    stats = jnp.concatenate(means + spreads, axis=0)
+    for i in range(num_dev):
+        out_ref[i, tile : tile + 2 * frames, 0:tile] = stats[:, i * tile : (i + 1) * tile]
 
 
 def local(
@@ -168,18 +190,16 @@
     sums = jnp.sum(scaled.reshape(patch, num_dev, feat), axis=2)
     base = jnp.sum(head_weight * mod_shift, axis=1) + head_bias
 
-    mine = lax.dynamic_slice_in_dim(scaled, dev_index * feat, feat, axis=1)
-    parts = jnp.einsum("fdt,kd->ftk", hidden, split3(mine), preferred_element_type=F32)
-    values = hidden.astype(F32)
-    mean = jnp.mean(values, axis=1)
-    centred = values - mean[:, None]
-    spread = jnp.sum(centred * centred, axis=1)
-    part = parts[..., :patch] + (parts[..., patch : 2 * patch] + parts[..., 2 * patch :])
-    part = part - mean[..., None] * jnp.sum(mine, axis=1)
-    part = part.reshape(frames, num_dev, tile, patch).transpose(1, 2, 0, 3).reshape(num_dev, tile, frames * patch)
-    stats = jnp.stack([mean, spread]).reshape(2 * frames, num_dev, tile).transpose(1, 0, 2)
-    stats = jnp.pad(stats, ((0, 0), (0, 8 - 2 * frames), (0, frames * patch - tile)))
-    sent = jnp.concatenate([part, stats], axis=1)
+    mine = lax.dynamic_slice_in_dim(head_weight, dev_index * feat, feat, axis=1)
+    mine = mine * (1.0 + lax.dynamic_slice_in_dim(mod_scale, dev_index * feat, feat))
+    vmem = pl.BlockSpec(memory_space=pltpu.VMEM)
+    sent = pl.pallas_call(
+        functools.partial(head_kernel, num_dev),
+        out_shape=jax.ShapeDtypeStruct((num_dev, tile + 8, frames * patch), F32),
+        in_specs=[vmem, vmem],
+        out_specs=vmem,
+        compiler_params=pltpu.CompilerParams(vmem_limit_bytes=40 * 1024 * 1024),
+    )(hidden, mine)
     got = lax.all_to_all(sent, "seq", split_axis=0, concat_axis=0, tiled=True)
 
     got_part = got[:, :tile].reshape(num_dev, tile, frames, patch)

time: 63.4 us -> 54.2 us (0.85)
  other arithmetic: 15.6 us -> 10.3 us
  local copies, waits for them, and re-layouts: 17.4 us -> 12.3 us
  Pallas kernels: 9.31 us -> 11.8 us
  waiting for transfers between devices: 7.27 us -> 6.49 us
  matrix products: 0.68 us -> 0 us
    reshape x4 -> x0, local copies, waits for them, and re-layouts: 4.42 us -> none  [the longest x2 3.17 us: local(): part.reshape(frames, num_dev, tile, patch).transpose(1, 2, 0, 3)]
    concatenate x2 -> x1, local copies, waits for them, and re-layouts: 2.69 us -> 0.16 us  [the longest x1 2.53 us: local(): sent = jnp.concatenate([part, stats], axis=1)]
    reduce_sum x3 -> x0, other arithmetic: 2.38 us -> none  [the longest x1 1.73 us: local(): mean = jnp.mean(values, axis=1)]
    pallas_call x0 -> x1, Pallas kernels: none -> 2.32 us  [local(): pl.pallas_call(functools.partial(head_kernel, num_dev), out_shape=jax.Sha...]
    concatenate x2 -> x1, other arithmetic: 2.4 us -> 0.1 us  [the longest x1 2.3 us: local(): sent = jnp.concatenate([part, stats], axis=1)]
    unnamed x29 -> x32, local copies, waits for them, and re-layouts: 3.24 us -> 5.11 us
    reduce_sum x1, other arithmetic: 1.58 us -> 0.25 us  [local(): base = jnp.sum(head_weight * mod_shift, axis=1) + head_bias]
    mul x0 -> x1, other arithmetic: none -> 0.99 us  [local(): mine * (1.0 + lax.dynamic_slice_in_dim(mod_scale, dev_index * feat, feat))]
  transfers between devices with their start and end apart: 3 -> 3, of which waited for: 2 -> 2; matrix products, arithmetic and copies ran while one was open for 18% -> 22% of each run, Pallas kernels for 0% -> 0%
where the time goes in v3:
time: 54.2 us; the launch traced here: 53.6 us
  starting transfers between devices  12.4 us (23%)
  local copies, waits for them, and re-layouts  12.3 us (23%)
  Pallas kernels  11.8 us (22%)
  other arithmetic  10.3 us (19%)
  waiting for transfers between devices  6.49 us (12%)
    pallas_call x1, Pallas kernels, decode(): pl.pallas_call(functools.partial(conv_kernel, num_dev, lat_rows, (c1, c2,...  9.5 us
    all_to_all x1, starting transfers between devices, local(): got = lax.all_to_all(sent, 'seq', split_axis=0, concat_axis=0, tiled=True)  6.65 us
    unnamed x32, local copies, waits for them, and re-layouts  5.11 us
    ppermute x1, waiting for transfers between devices, local(): high = lax.ppermute(projected[:, :1], 'seq', backward)  3.95 us
    ppermute x1, starting transfers between devices, local(): low = lax.ppermute(projected[:, -1:], 'seq', forward)  3.61 us
    all_to_all x1, waiting for transfers between devices, local(): got = lax.all_to_all(sent, 'seq', split_axis=0, concat_axis=0, tiled=True)  2.54 us
    pallas_call x1, Pallas kernels, local(): pl.pallas_call(functools.partial(head_kernel, num_dev), out_shape=jax.Sha...  2.32 us
    ppermute x1, starting transfers between devices, local(): high = lax.ppermute(projected[:, :1], 'seq', backward)  2.1 us
  transfers between devices with their start and end apart: 3, of which 2 were waited for; matrix products, arithmetic and copies ran while one was open for 22% of the time, Pallas kernels for 0%

profile of v3, /device:TPU:13, one launch (start us, length us, event | category | flops | bytes accessed | tf_op | source)
XLA Modules:
  0.0 53.6 jit_solution(17195974859288075234)
XLA Ops:
  0.0 0.8 %dynamic-slice_add_fusion = f32[320]{0:T(512)S(1)} fusion(f32[5120]{0:T(1024)} %param.15, s32[]{:T(128)S(6)} %select_n.4), kind=kLoop, calls=%fused_computation.40 | loop fusion | flops 320 | bytes 2564 | tf_op jit(solution)/shard_map/add | solution.py:194
  0.8 1.0 %dynamic-slice_multiply_fusion.w_ref = f32[64,320]{1,0:T(8,128)S(1)} fusion(f32[64,5120]{1,0:T(8,128)} %param.16, s32[]{:T(128)S(6)} %select_n.4, f32[320]{0:T(512)S(1)} %dynamic-slice_add_fusion), kind=kLoop, calls=%fused_computation.32 | loop fusion | flops 20480 | bytes 165124 | tf_op jit(solution)/shard_map/mul | solution.py:194
  1.8 0.0 copy-start.1
  1.8 1.4 %copy-done.1 = bf16[2,320,1280]{2,1,0:T(8,128)(2,1)S(1)} copy-done((bf16[2,320,1280]{2,1,0:T(8,128)(2,1)S(1)}, bf16[2,320,1280]{2,1,0:T(8,128)(2,1)}, u32[]{:S(2)}) %copy-start.1) | copy-done | bytes 1638424
  3.2 2.3 %shard_map.127 = f32[16,88,128]{2,1,0:T(8,128)} custom-call(bf16[2,320,1280]{2,1,0:T(8,128)(2,1)S(1)} %copy-done.1, f32[64,320]{1,0:T(8,128)S(1)} %dynamic-slice_multiply_fusion.w_ref), custom_call_target="tpu_custom_call" | custom-call | tf_op jit(solution)/shard_map/pallas_call | solution.py:196
  5.5 6.6 %all-to-all-start = ((f32[16,88,128]{2,1,0:T(8,128)}), f32[16,88,128]{2,1,0:T(8,128)}, u32[]{:S(2)}, u32[]{:S(2)}) async-start(f32[16,88,128]{2,1,0:T(8,128)} %shard_map.127), calls=%async_computation | async-start | bytes 1441792 | tf_op jit(solution)/shard_map/all_to_all | solution.py:203
  12.2 0.0 copy-done.10
  12.2 0.0 copy-done.5
  12.2 0.2 convert_element_type.17
  12.4 0.0 copy-start.9
  12.4 0.0 copy-start.11
  12.4 1.4 %slice_add_fusion.1 = (f32[1,3,384,192]{2,3,1,0:T(8,128)}, f32[1,3,384,192]{2,3,1,0:T(8,128)}) fusion(f32[3,3,384,192]{2,3,1,0:T(8,128)S(1)} %convert_element_type.17), kind=kLoop, calls=%fused_computation.20 | loop fusion | flops 442368 | bytes 4423680 | tf_op jit(solution)/shard_map/add | solution.py:118
  13.8 0.4 copy-done.9
  14.3 0.0 copy-done.11
  14.3 0.3 multiply_reduce_fusion
  14.5 1.3 %fusion.9 = (f32[1,3,384,192]{2,3,1,0:T(8,128)}, f32[1,3,384,192]{2,3,1,0:T(8,128)}) fusion(bf16[3,3,384,192]{2,3,1,0:T(8,128)(2,1)S(1)} %copy-done.5), kind=kLoop, calls=%fused_computation.46 | loop fusion | bytes 3538944 | tf_op jit(solution)/shard_map/slice | solution.py:118
  15.9 0.5 reshape.53
  16.4 0.0 copy-start.8
  16.4 0.2 reduce_sum.68
  16.6 0.1 copy.25
  16.6 0.9 %copy-done.8 = f32[1,3,384,192]{2,3,1,0:T(8,128)S(1)} copy-done((f32[1,3,384,192]{2,3,1,0:T(8,128)S(1)}, f32[1,3,384,192]{2,3,1,0:T(8,128)}, u32[]{:S(2)}) %copy-start.8) | copy-done | bytes 884760
  17.5 1.9 %maximum_bitcast_fusion = (f32[1,2,3,384,192]{3,4,2,1,0:T(8,128)S(1)}, f32[1,2,3,384,192]{3,4,2,1,0:T(8,128)S(1)}) fusion(f32[1,3,384,192]{2,3,1,0:T(8,128)} %get-tuple-element.13, f32[1,3,384,192]{2,3,1,0:T(8,128)S(1)} %copy-done.8, f32[1,3,384,192]{2,3,1,0:T(8,128)} %get-tuple-element.16, f32[1,3,384,192]{2,3,1,0:T(8,128)} %get-tuple-element.14), kind=kLoop, calls=%fused_computation.5 | loop fusion | flops 884736 | bytes 7077888 | tf_op jit(solution)/shard_map/stack | solution.py:117
  19.5 0.3 add_convert_fusion.1
  19.7 0.2 fusion.7
  19.9 0.1 pad_maximum_fusion.2
  20.1 1.6 %copy.27 = bf16[2,2,2,384,192]{4,3,2,1,0:T(8,128)(2,1)} copy(bf16[2,2,2,384,192]{3,4,2,1,0:T(8,128)(2,1)S(1)} %pad_maximum_fusion.2) | data formatting | bytes 2359296 | tf_op jit(solution)/shard_map/stack | solution.py:122
  21.7 0.1 pad_maximum_fusion.3
  21.8 1.6 %copy.28 = bf16[2,2,2,384,192]{4,3,2,1,0:T(8,128)(2,1)} copy(bf16[2,2,2,384,192]{3,4,2,1,0:T(8,128)(2,1)S(1)} %pad_maximum_fusion.3) | data formatting | bytes 2359296 | tf_op jit(solution)/shard_map/stack | solution.py:123
  23.4 0.7 %copy-done.14 = f32[64]{0:T(128)S(1)} copy-done((f32[64]{0:T(128)S(1)}, f32[64]{0:T(128)}, u32[]{:S(2)}) %copy-start.14) | copy-done | bytes 280
  24.1 0.5 slice-done
  24.6 0.3 pad_slice_fusion.5
  24.9 0.0 copy-start.6
  24.9 1.2 %pad_maximum_fusion.4.w3_ref = bf16[3,768,256]{2,1,0:T(8,128)(2,1)} fusion(bf16[3,768,128]{2,1,0:T(8,128)(2,1)S(1)} %bitcast.34, bf16[3,768,128]{2,1,0:T(8,128)(2,1)S(1)} %bitcast.33), kind=kLoop, calls=%fused_computation.15 | loop fusion | flops 2359296 | bytes 2359296 | tf_op jit(solution)/shard_map/concatenate | solution.py:129
  26.1 0.0 copy-done.7
  26.1 0.9 %copy-done.6 = bf16[2,2,2,384,192]{4,3,2,1,0:T(8,128)(2,1)S(1)} copy-done((bf16[2,2,2,384,192]{4,3,2,1,0:T(8,128)(2,1)S(1)}, bf16[2,2,2,384,192]{4,3,2,1,0:T(8,128)(2,1)}, u32[]{:S(2)}) %copy-start.6) | copy-done | bytes 1179672
  27.0 0.6 %pad_maximum_fusion.w2_ref = bf16[2,2,2,768,192]{4,3,2,1,0:T(8,128)(2,1)S(1)} fusion(bf16[2,2,1,768,192]{4,3,2,1,0:T(8,128)(2,1)S(1)} %bitcast.30, bf16[2,2,1,768,192]{4,3,2,1,0:T(8,128)(2,1)S(1)} %bitcast.29), kind=kLoop, calls=%fused_computation.4 | loop fusion | flops 1179648 | bytes 4718592 | tf_op jit(solution)/shard_map/stack | solution.py:120
  27.6 2.5 %all-to-all-done = f32[16,88,128]{2,1,0:T(8,128)} async-done(((f32[16,88,128]{2,1,0:T(8,128)}), f32[16,88,128]{2,1,0:T(8,128)}, u32[]{:S(2)}, u32[]{:S(2)}) %all-to-all-start) | async-done | bytes 720928 | tf_op jit(solution)/shard_map/all_to_all | solution.py:203
  30.1 0.8 %slice.87 = f32[16,4,80]{2,1,0:T(4,128)S(1)} slice(f32[16,88,128]{2,1,0:T(8,128)} %all-to-all-done), slice={[0:16], [80:84], [0:80]} | slice | bytes 40960 | tf_op jit(solution)/shard_map/slice | solution.py:206
  31.0 1.1 %slice_reduce_fusion = f32[80,128]{1,0:T(8,128)S(1)} fusion(f32[16,88,128]{2,1,0:T(8,128)} %all-to-all-done), kind=kLoop, calls=%fused_computation.21 | loop fusion | flops 153600 | bytes 696320 | tf_op jit(solution)/shard_map/reduce_sum | solution.py:212
  32.2 0.1 copy.24
  32.3 0.2 multiply_reduce_fusion.1
  32.5 0.1 fusion.6
  32.6 3.6 %collective-permute-start = (bf16[2,1,80,64]{2,3,0,1:T(8,128)(2,1)S(1)}, bf16[2,1,80,64]{2,3,0,1:T(8,128)(2,1)S(1)}, u32[]{:S(2)}, u32[]{:S(2)}) collective-permute-start(bf16[2,1,80,64]{2,3,0,1:T(8,128)(2,1)S(1)} %fusion.6), channel_id=1, source_target_pairs={{0,1},{1,2},{2,3},{3,4},{4,5},{5,6},{6,7},{7,8},{8,9},{9,10},{10,1... | collective-permute-start | bytes 61448 | tf_op jit(solution)/shard_map/ppermute | solution.py:218
  36.2 2.1 %collective-permute-start.1 = (bf16[2,1,80,64]{2,3,0,1:T(8,128)(2,1)S(1)}, bf16[2,1,80,64]{2,3,0,1:T(8,128)(2,1)S(1)}, u32[]{:S(2)}, u32[]{:S(2)}) collective-permute-start(bf16[2,1,80,64]{2,3,0,1:T(8,128)(2,1)S(1)} %fusion.6), channel_id=1, source_target_pairs={{1,0},{2,1},{3,2},{4,3},{5,4},{6,5},{7,6},{8,7},{9,8},{10,9},{11,1... | collective-permute-start | bytes 61448 | tf_op jit(solution)/shard_map/ppermute | solution.py:219
  38.3 0.0 copy-done.15
  38.3 0.0 copy-done.12
  38.3 0.0 copy-done.13
  38.3 0.0 collective-permute-done
  38.4 3.9 %collective-permute-done.1 = bf16[2,1,80,64]{2,3,0,1:T(8,128)(2,1)S(1)} collective-permute-done((bf16[2,1,80,64]{2,3,0,1:T(8,128)(2,1)S(1)}, bf16[2,1,80,64]{2,3,0,1:T(8,128)(2,1)S(1)}, u32[]{:S(2)}, u32[]{:S(2)}) %collective-permute-start.1) | collective-permute-done | bytes 20512 | tf_op jit(solution)/shard_map/ppermute | solution.py:219
  42.4 0.1 pad_maximum_fusion.7
  42.5 0.2 copy.26
  42.6 0.2 fusion.11
  42.8 0.0 copy-start
  42.8 0.0 copy-start.2
  42.8 0.0 copy-start.3
  42.8 0.0 copy-start.4
  42.8 0.3 fusion.4
  43.1 0.1 fusion.10
  43.2 0.2 pad_maximum_fusion.5.x_ref
  43.4 0.7 %copy-done = bf16[3,768,256]{2,1,0:T(8,128)(2,1)S(1)} copy-done((bf16[3,768,256]{2,1,0:T(8,128)(2,1)S(1)}, bf16[3,768,256]{2,1,0:T(8,128)(2,1)}, u32[]{:S(2)}) %copy-start) | copy-done | bytes 1179672
  44.1 0.1 copy-done.2
  44.1 0.0 copy-done.3
  44.1 0.0 copy-done.4
  44.1 9.5 %shard_map.128 = bf16[8,96,320]{2,1,0:T(8,128)(2,1)} custom-call(s32[1]{0:T(128)} %bitcast.pos_ref, bf16[2,4,80,192]{3,2,1,0:T(8,128)(2,1)S(1)} %pad_maximum_fusion.5.x_ref, bf16[3,3,3,16,384]{4,3,2,1,0:T(8,128)(2,1)S(1)} %copy-done.2, f32[1,384]{1,0:T(1,128)S(1)} %broadcast_in_dim.13.b1_ref, f32[1,384]{1,0:T(1,128)S(1)} %broadcast_in_dim.28.g1_ref, ...), custom_call_target="tpu_custom_call" | custom-call | tf_op jit(solution)/shard_map/pallas_call | solution.py:133
  (19 shorter events, 0.1 us)
Async XLA Ops:
  1.8 1.4 %copy-start.1 = (bf16[2,320,1280]{2,1,0:T(8,128)(2,1)S(1)}, bf16[2,320,1280]{2,1,0:T(8,128)(2,1)}, u32[]{:S(2)}) copy-start(bf16[2,320,1280]{2,1,0:T(8,128)(2,1)} %x_ref.1) | copy-start | bytes 4915204
  5.5 6.7 %copy-start.10 = (f32[5120]{0:T(1024)S(1)}, f32[5120]{0:T(1024)}, u32[]{:S(2)}) copy-start(f32[5120]{0:T(1024)} %param.15) | copy-start | bytes 61444
  5.5 6.7 %copy-start.5 = (bf16[3,3,384,192]{2,3,1,0:T(8,128)(2,1)S(1)}, bf16[3,3,384,192]{2,3,1,0:T(8,128)(2,1)}, u32[]{:S(2)}) copy-start(bf16[3,3,384,192]{2,3,1,0:T(8,128)(2,1)} %param.21) | copy-start | bytes 3981316
  5.5 24.6 %all-to-all-start = ((f32[16,88,128]{2,1,0:T(8,128)}), f32[16,88,128]{2,1,0:T(8,128)}, u32[]{:S(2)}, u32[]{:S(2)}) async-start(f32[16,88,128]{2,1,0:T(8,128)} %shard_map.127), calls=%async_computation | async-start | bytes 1441792 | tf_op jit(solution)/shard_map/all_to_all | solution.py:203
  12.4 1.8 %copy-start.9 = (f32[64,5120]{1,0:T(8,128)S(1)}, f32[64,5120]{1,0:T(8,128)}, u32[]{:S(2)}) copy-start(f32[64,5120]{1,0:T(8,128)} %param.16) | copy-start | bytes 3932164
  12.4 1.8 %copy-start.11 = (f32[5120]{0:T(1024)S(1)}, f32[5120]{0:T(1024)}, u32[]{:S(2)}) copy-start(f32[5120]{0:T(1024)} %param.14) | copy-start | bytes 61444
  16.4 1.2 %copy-start.8 = (f32[1,3,384,192]{2,3,1,0:T(8,128)S(1)}, f32[1,3,384,192]{2,3,1,0:T(8,128)}, u32[]{:S(2)}) copy-start(f32[1,3,384,192]{2,3,1,0:T(8,128)} %get-tuple-element.15) | copy-start | bytes 2654212
  23.4 0.7 %copy-start.14 = (f32[64]{0:T(128)S(1)}, f32[64]{0:T(128)}, u32[]{:S(2)}) copy-start(f32[64]{0:T(128)} %param.17) | copy-start | bytes 772
  23.4 1.2 %slice-start = ((bf16[3,3,3,192,96]{4,3,2,1,0:T(8,128)(2,1)}), bf16[2,3,3,192,96]{4,3,2,1,0:T(8,128)(2,1)S(1)}, s32[]{:S(2)}) async-start(bf16[3,3,3,192,96]{4,3,2,1,0:T(8,128)(2,1)} %param.24), calls=%async_computation.1 | async-start | bytes 1769472 | tf_op jit(solution)/shard_map/slice | solution.py:128
  24.6 1.5 %copy-start.7 = (bf16[2,2,2,384,192]{4,3,2,1,0:T(8,128)(2,1)S(1)}, bf16[2,2,2,384,192]{4,3,2,1,0:T(8,128)(2,1)}, u32[]{:S(2)}) copy-start(bf16[2,2,2,384,192]{4,3,2,1,0:T(8,128)(2,1)} %copy.28) | copy-start | bytes 3538948
  24.9 2.1 %copy-start.6 = (bf16[2,2,2,384,192]{4,3,2,1,0:T(8,128)(2,1)S(1)}, bf16[2,2,2,384,192]{4,3,2,1,0:T(8,128)(2,1)}, u32[]{:S(2)}) copy-start(bf16[2,2,2,384,192]{4,3,2,1,0:T(8,128)(2,1)} %copy.27) | copy-start | bytes 3538948
  27.0 11.3 %copy-start.15 = (f32[96]{0:T(128)S(1)}, f32[96]{0:T(128)}, u32[]{:S(2)}) copy-start(f32[96]{0:T(128)} %param.25) | copy-start | bytes 1156
  27.0 11.3 %copy-start.12 = (f32[384]{0:T(512)S(1)}, f32[384]{0:T(512)}, u32[]{:S(2)}) copy-start(f32[384]{0:T(512)} %param.19) | copy-start | bytes 4612
  27.0 11.4 %copy-start.13 = (f32[384]{0:T(512)S(1)}, f32[384]{0:T(512)}, u32[]{:S(2)}) copy-start(f32[384]{0:T(512)} %param.20) | copy-start | bytes 4612
  32.6 5.8 %collective-permute-start = (bf16[2,1,80,64]{2,3,0,1:T(8,128)(2,1)S(1)}, bf16[2,1,80,64]{2,3,0,1:T(8,128)(2,1)S(1)}, u32[]{:S(2)}, u32[]{:S(2)}) collective-permute-start(bf16[2,1,80,64]{2,3,0,1:T(8,128)(2,1)S(1)} %fusion.6), channel_id=1, source_target_pairs={{0,1},{1,2},{2,3},{3,4},{4,5},{5,6},{6,7},{7,8},{8,9},{9,10},{10,1... | collective-permute-start | bytes 61448 | tf_op jit(solution)/shard_map/ppermute | solution.py:218
  36.2 6.1 %collective-permute-start.1 = (bf16[2,1,80,64]{2,3,0,1:T(8,128)(2,1)S(1)}, bf16[2,1,80,64]{2,3,0,1:T(8,128)(2,1)S(1)}, u32[]{:S(2)}, u32[]{:S(2)}) collective-permute-start(bf16[2,1,80,64]{2,3,0,1:T(8,128)(2,1)S(1)} %fusion.6), channel_id=1, source_target_pairs={{1,0},{2,1},{3,2},{4,3},{5,4},{6,5},{7,6},{8,7},{9,8},{10,9},{11,1... | collective-permute-start | bytes 61448 | tf_op jit(solution)/shard_map/ppermute | solution.py:219
  42.8 1.3 %copy-start = (bf16[3,768,256]{2,1,0:T(8,128)(2,1)S(1)}, bf16[3,768,256]{2,1,0:T(8,128)(2,1)}, u32[]{:S(2)}) copy-start(bf16[3,768,256]{2,1,0:T(8,128)(2,1)} %pad_maximum_fusion.4.w3_ref) | copy-start | bytes 3538948
  42.8 1.3 %copy-start.2 = (bf16[3,3,3,16,384]{4,3,2,1,0:T(8,128)(2,1)S(1)}, bf16[3,3,3,16,384]{4,3,2,1,0:T(8,128)(2,1)}, u32[]{:S(2)}) copy-start(bf16[3,3,3,16,384]{4,3,2,1,0:T(8,128)(2,1)} %w1_ref.1) | copy-start | bytes 995332
  42.8 1.3 %copy-start.3 = (f32[192]{0:T(256)S(1)}, f32[192]{0:T(256)}, u32[]{:S(2)}) copy-start(f32[192]{0:T(256)} %param.22) | copy-start | bytes 2308
  42.8 1.3 %copy-start.4 = (f32[192]{0:T(256)S(1)}, f32[192]{0:T(256)}, u32[]{:S(2)}) copy-start(f32[192]{0:T(256)} %param.23) | copy-start | bytes 2308

commit v4 on v3

--- a/solution.py
+++ b/solution.py
@@ -175,6 +175,20 @@
         out_ref[i, tile : tile + 2 * frames, 0:tile] = stats[:, i * tile : (i + 1) * tile]
 
 
+def merge_kernel(feat, tile, got_ref, sums_ref, base_ref, out_ref):
+    num_dev = got_ref.shape[0]
+    patch = sums_ref.shape[1]
+    for f in range(2):
+        means = got_ref[:, tile + f, :]
+        off = means - jnp.mean(means, axis=0, keepdims=True)
+        spread = jnp.sum(got_ref[:, tile + 2 + f, :], axis=0, keepdims=True)
+        var = (spread + feat * jnp.sum(off * off, axis=0, keepdims=True)) * (1.0 / (feat * num_dev))
+        scale = jnp.transpose(jnp.broadcast_to(lax.rsqrt(var + 1e-06), (8, var.shape[1])))[0:tile, 0:1]
+        fixed = jnp.dot(jnp.transpose(off), sums_ref[...], precision=HIGH, preferred_element_type=F32)
+        summed = jnp.sum(got_ref[:, 0:tile, :], axis=0)[:, f * patch : (f + 1) * patch] + fixed[0:tile]
+        out_ref[f] = (summed * scale + base_ref[...]).astype(BF16)
+
+
 def local(
     hidden, mod_shift, mod_scale, head_weight, head_bias, conv_in_weight, conv_in_bias, gain_in,
     up_weight, up_bias, gain_up, out_weight, out_bias,
@@ -202,15 +216,13 @@
     )(hidden, mine)
     got = lax.all_to_all(sent, "seq", split_axis=0, concat_axis=0, tiled=True)
 
-    got_part = got[:, :tile].reshape(num_dev, tile, frames, patch)
-    got_stat = got[:, tile : tile + 2 * frames, :tile].reshape(num_dev, 2, frames, tile)
-    means = got_stat[:, 0]
-    total_mean = jnp.mean(means, axis=0)
-    off = means - total_mean
-    var = (jnp.sum(got_stat[:, 1], axis=0) + feat * jnp.sum(off * off, axis=0)) / (feat * num_dev)
-    fixed = jnp.sum(off[..., None] * sums.T[:, None, None, :], axis=0)
-    summed = jnp.sum(got_part, axis=0).transpose(1, 0, 2) + fixed
-    projected = (summed * lax.rsqrt(var + 1e-06)[..., None] + base).astype(BF16)
+    projected = pl.pallas_call(
+        functools.partial(merge_kernel, feat, tile),
+        out_shape=jax.ShapeDtypeStruct((frames, tile, patch), BF16),
+        in_specs=[vmem] * 3,
+        out_specs=vmem,
+        compiler_params=pltpu.CompilerParams(vmem_limit_bytes=40 * 1024 * 1024),
+    )(got, sums.T, base[None])
     projected = projected.reshape(frames, rows_dev, TOK_W, patch)
 
     forward = [(i, i + 1) for i in range(num_dev - 1)]

time: 54.2 us -> 53.2 us (0.982)
  Pallas kernels: 11.8 us -> 13.3 us
  waiting for transfers between devices: 6.49 us -> 5.27 us
  local copies, waits for them, and re-layouts: 12.3 us -> 11.5 us
    another operation x2, other arithmetic: 0.45 us -> 2.2 us
    pallas_call x0 -> x1, Pallas kernels: none -> 1.61 us  [local(): pl.pallas_call(functools.partial(merge_kernel, feat, tile), out_shape=jax...]
    reduce_sum x4 -> x0, other arithmetic: 1.39 us -> none  [the longest x1 1.13 us: local(): summed = jnp.sum(got_part, axis=0).transpose(1, 0, 2) + fixed]
    all_to_all x1, waiting for transfers between devices: 2.54 us -> 1.23 us  [local(): got = lax.all_to_all(sent, 'seq', split_axis=0, concat_axis=0, tiled=True)]
    reshape x1, local copies, waits for them, and re-layouts: 0.49 us -> 1.74 us  [local(): sums = jnp.sum(scaled.reshape(patch, num_dev, feat), axis=2)]
    add x1, other arithmetic: 1.38 us -> 0.15 us  [decode(): wide[1] + wide[2]]
    slice x1, local copies, waits for them, and re-layouts: 1.34 us -> 0.12 us  [decode(): wide[0]]
    reduce_sum x1, other arithmetic: 0.25 us -> 1.31 us  [local(): base = jnp.sum(head_weight * mod_shift, axis=1) + head_bias]
  transfers between devices with their start and end apart: 3 -> 3, of which waited for: 2 -> 2; matrix products, arithmetic and copies ran while one was open for 22% -> 25% of each run, Pallas kernels for 0% -> 0%
where the time goes in v4:
time: 53.2 us; the launch traced here: 52.7 us
  Pallas kernels  13.3 us (25%)
  starting transfers between devices  12.4 us (23%)
  local copies, waits for them, and re-layouts  11.5 us (22%)
  other arithmetic  9.95 us (19%)
  waiting for transfers between devices  5.27 us (10%)
    pallas_call x1, Pallas kernels, decode(): pl.pallas_call(functools.partial(conv_kernel, num_dev, lat_rows, (c1, c2,...  9.42 us
    all_to_all x1, starting transfers between devices, local(): got = lax.all_to_all(sent, 'seq', split_axis=0, concat_axis=0, tiled=True)  6.65 us
    unnamed x32, local copies, waits for them, and re-layouts  4.54 us
    ppermute x1, waiting for transfers between devices, local(): high = lax.ppermute(projected[:, :1], 'seq', backward)  4.04 us
    ppermute x1, starting transfers between devices, local(): low = lax.ppermute(projected[:, -1:], 'seq', forward)  3.61 us
    pallas_call x1, Pallas kernels, local(): pl.pallas_call(functools.partial(head_kernel, num_dev), out_shape=jax.Sha...  2.31 us
    another operation x2, other arithmetic  2.2 us
    ppermute x1, starting transfers between devices, local(): high = lax.ppermute(projected[:, :1], 'seq', backward)  2.1 us
  transfers between devices with their start and end apart: 3, of which 2 were waited for; matrix products, arithmetic and copies ran while one was open for 25% of the time, Pallas kernels for 0%

profile of v4, /device:TPU:13, one launch (start us, length us, event | category | flops | bytes accessed | tf_op | source)
XLA Modules:
  0.0 52.7 jit_solution(14118774584412655586)
XLA Ops:
  0.0 0.8 %dynamic-slice_add_fusion = f32[320]{0:T(512)S(1)} fusion(f32[5120]{0:T(1024)} %param.15, s32[]{:T(128)S(6)} %select_n.4), kind=kLoop, calls=%fused_computation.32 | loop fusion | flops 320 | bytes 2564 | tf_op jit(solution)/shard_map/add | solution.py:208
  0.8 1.0 %dynamic-slice_multiply_fusion.w_ref = f32[64,320]{1,0:T(8,128)S(1)} fusion(f32[64,5120]{1,0:T(8,128)} %param.16, s32[]{:T(128)S(6)} %select_n.4, f32[320]{0:T(512)S(1)} %dynamic-slice_add_fusion), kind=kLoop, calls=%fused_computation.30 | loop fusion | flops 20480 | bytes 165124 | tf_op jit(solution)/shard_map/mul | solution.py:208
  1.8 0.0 copy-start.1
  1.8 1.4 %copy-done.1 = bf16[2,320,1280]{2,1,0:T(8,128)(2,1)S(1)} copy-done((bf16[2,320,1280]{2,1,0:T(8,128)(2,1)S(1)}, bf16[2,320,1280]{2,1,0:T(8,128)(2,1)}, u32[]{:S(2)}) %copy-start.1) | copy-done | bytes 1638424
  3.2 2.3 %shard_map.127 = f32[16,88,128]{2,1,0:T(8,128)} custom-call(bf16[2,320,1280]{2,1,0:T(8,128)(2,1)S(1)} %copy-done.1, f32[64,320]{1,0:T(8,128)S(1)} %dynamic-slice_multiply_fusion.w_ref), custom_call_target="tpu_custom_call" | custom-call | tf_op jit(solution)/shard_map/pallas_call | solution.py:210
  5.5 0.0 copy-start.10
  5.5 0.0 copy-start.6
  5.5 6.6 %all-to-all-start = ((f32[16,88,128]{2,1,0:T(8,128)}), f32[16,88,128]{2,1,0:T(8,128)}, u32[]{:S(2)}, u32[]{:S(2)}) async-start(f32[16,88,128]{2,1,0:T(8,128)} %shard_map.127), calls=%async_computation | async-start | bytes 1441792 | tf_op jit(solution)/shard_map/all_to_all | solution.py:217
  12.2 0.0 copy-done.10
  12.2 0.0 copy-done.6
  12.2 0.2 convert_element_type.13
  12.4 0.1 fusion.8
  12.5 0.0 copy-start.9
  12.5 0.0 copy-start.11
  12.6 0.1 slice_add_fusion.1
  12.7 1.1 %copy-done.9 = f32[64,5120]{1,0:T(8,128)S(1)} copy-done((f32[64,5120]{1,0:T(8,128)S(1)}, f32[64,5120]{1,0:T(8,128)}, u32[]{:S(2)}) %copy-start.9) | copy-done | bytes 1310744
  13.9 0.0 copy-done.11
  13.9 1.3 %multiply_reduce_fusion = (f32[64]{0:T(128)S(1)}, f32[64,5120]{1,0:T(8,128)}) fusion(f32[64,5120]{1,0:T(8,128)S(1)} %copy-done.9, f32[5120]{0:T(1024)S(1)} %copy-done.11, f32[5120]{0:T(1024)S(1)} %broadcast_add_fusion), kind=kLoop, calls=%fused_computation.7 | loop fusion | flops 982976 | bytes 2662656 | tf_op jit(solution)/shard_map/reduce_sum | solution.py:205
  15.2 1.5 %maximum_bitcast_fusion = (f32[1,2,3,384,192]{3,4,2,1,0:T(8,128)S(1)}, f32[1,2,3,384,192]{3,4,2,1,0:T(8,128)}) fusion(f32[1,3,384,192]{2,3,1,0:T(8,128)S(1)} %get-tuple-element.9, f32[1,3,384,192]{2,3,1,0:T(8,128)S(1)} %get-tuple-element.11, f32[1,3,384,192]{2,3,1,0:T(8,128)S(1)} %get-tuple-element.12, f32[1,3,384,192]{2,3,1,0:T(8,128)S(1)} %get-tuple-element.10), kind=kLoop, calls=%fused_computation.5 | loop fusion | flops 884736 | bytes 7077888 | tf_op jit(solution)/shard_map/stack | solution.py:117
  16.7 1.7 %reshape.28 = f32[64,16,320]{2,1,0:T(8,128)S(1)} reshape(f32[64,5120]{1,0:T(8,128)} %get-tuple-element.14) | data formatting | bytes 2621440 | tf_op jit(solution)/shard_map/reshape | solution.py:204
  18.4 0.2 reduce_sum.18
  18.7 0.1 copy.23
  18.7 0.0 copy-start.5
  18.7 2.0 %add_convert_fusion.1 = (bf16[2,2,1,384,192]{3,4,2,1,0:T(8,128)(2,1)S(1)}, bf16[2,2,1,384,192]{3,4,2,1,0:T(8,128)(2,1)S(1)}) fusion(f32[1,2,3,384,192]{3,4,2,1,0:T(8,128)} %get-tuple-element.25, f32[1,2,3,384,192]{3,4,2,1,0:T(8,128)S(1)} %get-tuple-element.24), kind=kLoop, calls=%fused_computation.17 | loop fusion | flops 2359296 | bytes 4718592 | tf_op jit(solution)/shard_map/convert.7
  20.7 0.2 copy-done.5
  20.9 0.2 fusion.6
  21.1 0.1 pad_maximum_fusion.2
  21.3 1.6 %copy.25 = bf16[2,2,2,384,192]{4,3,2,1,0:T(8,128)(2,1)} copy(bf16[2,2,2,384,192]{3,4,2,1,0:T(8,128)(2,1)S(1)} %pad_maximum_fusion.2) | data formatting | bytes 2359296 | tf_op jit(solution)/shard_map/stack | solution.py:122
  22.9 0.1 pad_maximum_fusion.3
  23.1 1.6 %copy.26 = bf16[2,2,2,384,192]{4,3,2,1,0:T(8,128)(2,1)} copy(bf16[2,2,2,384,192]{3,4,2,1,0:T(8,128)(2,1)S(1)} %pad_maximum_fusion.3) | data formatting | bytes 2359296 | tf_op jit(solution)/shard_map/stack | solution.py:123
  24.7 1.2 %slice-done = bf16[2,3,3,192,96]{4,3,2,1,0:T(8,128)(2,1)S(1)} async-done(((bf16[3,3,3,192,96]{4,3,2,1,0:T(8,128)(2,1)}), bf16[2,3,3,192,96]{4,3,2,1,0:T(8,128)(2,1)S(1)}, s32[]{:S(2)}) %slice-start) | async-done | bytes 663576 | tf_op jit(solution)/shard_map/slice | solution.py:128
  25.8 0.0 copy-start.8
  25.8 0.3 pad_slice_fusion.5
  26.1 0.0 copy-start.7
  26.1 1.2 %pad_maximum_fusion.4.w3_ref = bf16[3,768,256]{2,1,0:T(8,128)(2,1)} fusion(bf16[3,768,128]{2,1,0:T(8,128)(2,1)S(1)} %bitcast.32, bf16[3,768,128]{2,1,0:T(8,128)(2,1)S(1)} %bitcast.31), kind=kLoop, calls=%fused_computation.15 | loop fusion | flops 2359296 | bytes 2359296 | tf_op jit(solution)/shard_map/concatenate | solution.py:129
  27.3 0.0 copy-done.8
  27.3 0.9 %copy-done.7 = bf16[2,2,2,384,192]{4,3,2,1,0:T(8,128)(2,1)S(1)} copy-done((bf16[2,2,2,384,192]{4,3,2,1,0:T(8,128)(2,1)S(1)}, bf16[2,2,2,384,192]{4,3,2,1,0:T(8,128)(2,1)}, u32[]{:S(2)}) %copy-start.7) | copy-done | bytes 1179672
  28.2 0.0 copy-start.14
  28.2 0.6 %pad_maximum_fusion.w2_ref = bf16[2,2,2,768,192]{4,3,2,1,0:T(8,128)(2,1)S(1)} fusion(bf16[2,2,1,768,192]{4,3,2,1,0:T(8,128)(2,1)S(1)} %bitcast.28, bf16[2,2,1,768,192]{4,3,2,1,0:T(8,128)(2,1)S(1)} %bitcast.27), kind=kLoop, calls=%fused_computation.4 | loop fusion | flops 1179648 | bytes 4718592 | tf_op jit(solution)/shard_map/stack | solution.py:120
  28.8 0.0 copy-done.14
  28.9 1.2 %all-to-all-done.got_ref = f32[16,88,128]{2,1,0:T(8,128)} async-done(((f32[16,88,128]{2,1,0:T(8,128)}), f32[16,88,128]{2,1,0:T(8,128)}, u32[]{:S(2)}, u32[]{:S(2)}) %all-to-all-start) | async-done | bytes 720928 | tf_op jit(solution)/shard_map/all_to_all | solution.py:217
  30.1 1.6 %shard_map.128 = bf16[2,80,64]{2,1,0:T(8,128)(2,1)S(1)} custom-call(f32[16,88,128]{2,1,0:T(8,128)} %all-to-all-done.got_ref, f32[16,64]{1,0:T(8,128)S(1)} %bitcast.24, f32[1,64]{1,0:T(1,128)S(1)} %add_bitcast_fusion.base_ref), custom_call_target="tpu_custom_call" | custom-call | tf_op jit(solution)/shard_map/pallas_call | solution.py:219
  31.7 3.6 %collective-permute-start = (bf16[2,1,80,64]{3,2,0,1:T(8,128)(2,1)S(1)}, bf16[2,1,80,64]{3,2,0,1:T(8,128)(2,1)S(1)}, u32[]{:S(2)}, u32[]{:S(2)}) collective-permute-start(bf16[2,1,80,64]{3,2,0,1:T(8,128)(2,1)S(1)} %bitcast.21), channel_id=1, source_target_pairs={{0,1},{1,2},{2,3},{3,4},{4,5},{5,6},{6,7},{7,8},{8,9},{9,10},{10,1... | collective-permute-start | bytes 61448 | tf_op jit(solution)/shard_map/ppermute | solution.py:230
  35.3 2.1 %collective-permute-start.1 = (bf16[2,1,80,64]{3,2,0,1:T(8,128)(2,1)S(1)}, bf16[2,1,80,64]{3,2,0,1:T(8,128)(2,1)S(1)}, u32[]{:S(2)}, u32[]{:S(2)}) collective-permute-start(bf16[2,1,80,64]{3,2,0,1:T(8,128)(2,1)S(1)} %bitcast.22), channel_id=1, source_target_pairs={{1,0},{2,1},{3,2},{4,3},{5,4},{6,5},{7,6},{8,7},{9,8},{10,9},{11,1... | collective-permute-start | bytes 61448 | tf_op jit(solution)/shard_map/ppermute | solution.py:231
  37.4 0.0 copy-done.15
  37.5 0.0 copy-done.12
  37.5 0.0 copy-done.13
  37.5 0.0 collective-permute-done
  37.5 4.0 %collective-permute-done.1 = bf16[2,1,80,64]{3,2,0,1:T(8,128)(2,1)S(1)} collective-permute-done((bf16[2,1,80,64]{3,2,0,1:T(8,128)(2,1)S(1)}, bf16[2,1,80,64]{3,2,0,1:T(8,128)(2,1)S(1)}, u32[]{:S(2)}, u32[]{:S(2)}) %collective-permute-start.1) | collective-permute-done | bytes 20512 | tf_op jit(solution)/shard_map/ppermute | solution.py:231
  41.6 0.1 fusion.11
  41.7 0.1 pad_maximum_fusion.6
  41.8 0.2 fusion.10
  41.9 0.0 copy-start
  42.0 0.0 copy-start.2
  42.0 0.0 copy-start.3
  42.0 0.0 copy-start.4
  42.0 0.3 fusion.4
  42.3 0.1 fusion.9
  42.4 0.2 pad_maximum_fusion.5.x_ref
  42.5 0.7 %copy-done = bf16[3,768,256]{2,1,0:T(8,128)(2,1)S(1)} copy-done((bf16[3,768,256]{2,1,0:T(8,128)(2,1)S(1)}, bf16[3,768,256]{2,1,0:T(8,128)(2,1)}, u32[]{:S(2)}) %copy-start) | copy-done | bytes 1179672
  43.2 0.1 copy-done.2
  43.3 0.0 copy-done.3
  43.3 0.0 copy-done.4
  43.3 9.4 %shard_map.129 = bf16[8,96,320]{2,1,0:T(8,128)(2,1)} custom-call(s32[1]{0:T(128)} %bitcast.pos_ref, bf16[2,4,80,192]{3,2,1,0:T(8,128)(2,1)S(1)} %pad_maximum_fusion.5.x_ref, bf16[3,3,3,16,384]{4,3,2,1,0:T(8,128)(2,1)S(1)} %copy-done.2, f32[1,384]{1,0:T(1,128)S(1)} %broadcast_in_dim.26.b1_ref, f32[1,384]{1,0:T(1,128)S(1)} %broadcast_in_dim.27.g1_ref, ...), custom_call_target="tpu_custom_call" | custom-call | tf_op jit(solution)/shard_map/pallas_call | solution.py:133
  (11 shorter events, 0.1 us)
Async XLA Ops:
  1.8 1.4 %copy-start.1 = (bf16[2,320,1280]{2,1,0:T(8,128)(2,1)S(1)}, bf16[2,320,1280]{2,1,0:T(8,128)(2,1)}, u32[]{:S(2)}) copy-start(bf16[2,320,1280]{2,1,0:T(8,128)(2,1)} %x_ref.1) | copy-start | bytes 4915204
  5.5 6.7 %copy-start.10 = (f32[5120]{0:T(1024)S(1)}, f32[5120]{0:T(1024)}, u32[]{:S(2)}) copy-start(f32[5120]{0:T(1024)} %param.15) | copy-start | bytes 61444
  5.5 6.7 %copy-start.6 = (bf16[3,3,384,192]{2,3,1,0:T(8,128)(2,1)S(1)}, bf16[3,3,384,192]{2,3,1,0:T(8,128)(2,1)}, u32[]{:S(2)}) copy-start(bf16[3,3,384,192]{2,3,1,0:T(8,128)(2,1)} %param.21) | copy-start | bytes 3981316
  5.5 24.6 %all-to-all-start = ((f32[16,88,128]{2,1,0:T(8,128)}), f32[16,88,128]{2,1,0:T(8,128)}, u32[]{:S(2)}, u32[]{:S(2)}) async-start(f32[16,88,128]{2,1,0:T(8,128)} %shard_map.127), calls=%async_computation | async-start | bytes 1441792 | tf_op jit(solution)/shard_map/all_to_all | solution.py:217
  12.5 1.3 %copy-start.9 = (f32[64,5120]{1,0:T(8,128)S(1)}, f32[64,5120]{1,0:T(8,128)}, u32[]{:S(2)}) copy-start(f32[64,5120]{1,0:T(8,128)} %param.16) | copy-start | bytes 3932164
  12.5 1.3 %copy-start.11 = (f32[5120]{0:T(1024)S(1)}, f32[5120]{0:T(1024)}, u32[]{:S(2)}) copy-start(f32[5120]{0:T(1024)} %param.14) | copy-start | bytes 61444
  18.7 2.2 %copy-start.5 = (f32[1,2,3,384,192]{3,4,2,1,0:T(8,128)S(1)}, f32[1,2,3,384,192]{3,4,2,1,0:T(8,128)}, u32[]{:S(2)}) copy-start(f32[1,2,3,384,192]{3,4,2,1,0:T(8,128)} %get-tuple-element.25) | copy-start | bytes 5308420
  24.7 1.2 %slice-start = ((bf16[3,3,3,192,96]{4,3,2,1,0:T(8,128)(2,1)}), bf16[2,3,3,192,96]{4,3,2,1,0:T(8,128)(2,1)S(1)}, s32[]{:S(2)}) async-start(bf16[3,3,3,192,96]{4,3,2,1,0:T(8,128)(2,1)} %param.24), calls=%async_computation.1 | async-start | bytes 1769472 | tf_op jit(solution)/shard_map/slice | solution.py:128
  25.8 1.5 %copy-start.8 = (bf16[2,2,2,384,192]{4,3,2,1,0:T(8,128)(2,1)S(1)}, bf16[2,2,2,384,192]{4,3,2,1,0:T(8,128)(2,1)}, u32[]{:S(2)}) copy-start(bf16[2,2,2,384,192]{4,3,2,1,0:T(8,128)(2,1)} %copy.26) | copy-start | bytes 3538948
  26.1 2.1 %copy-start.7 = (bf16[2,2,2,384,192]{4,3,2,1,0:T(8,128)(2,1)S(1)}, bf16[2,2,2,384,192]{4,3,2,1,0:T(8,128)(2,1)}, u32[]{:S(2)}) copy-start(bf16[2,2,2,384,192]{4,3,2,1,0:T(8,128)(2,1)} %copy.25) | copy-start | bytes 3538948
  28.2 0.7 %copy-start.14 = (f32[64]{0:T(128)S(1)}, f32[64]{0:T(128)}, u32[]{:S(2)}) copy-start(f32[64]{0:T(128)} %param.17) | copy-start | bytes 772
  28.2 9.2 %copy-start.15 = (f32[96]{0:T(128)S(1)}, f32[96]{0:T(128)}, u32[]{:S(2)}) copy-start(f32[96]{0:T(128)} %param.25) | copy-start | bytes 1156
  28.2 9.2 %copy-start.12 = (f32[384]{0:T(512)S(1)}, f32[384]{0:T(512)}, u32[]{:S(2)}) copy-start(f32[384]{0:T(512)} %param.19) | copy-start | bytes 4612
  28.2 9.3 %copy-start.13 = (f32[384]{0:T(512)S(1)}, f32[384]{0:T(512)}, u32[]{:S(2)}) copy-start(f32[384]{0:T(512)} %param.20) | copy-start | bytes 4612
  31.7 5.8 %collective-permute-start = (bf16[2,1,80,64]{3,2,0,1:T(8,128)(2,1)S(1)}, bf16[2,1,80,64]{3,2,0,1:T(8,128)(2,1)S(1)}, u32[]{:S(2)}, u32[]{:S(2)}) collective-permute-start(bf16[2,1,80,64]{3,2,0,1:T(8,128)(2,1)S(1)} %bitcast.21), channel_id=1, source_target_pairs={{0,1},{1,2},{2,3},{3,4},{4,5},{5,6},{6,7},{7,8},{8,9},{9,10},{10,1... | collective-permute-start | bytes 61448 | tf_op jit(solution)/shard_map/ppermute | solution.py:230
  35.3 6.2 %collective-permute-start.1 = (bf16[2,1,80,64]{3,2,0,1:T(8,128)(2,1)S(1)}, bf16[2,1,80,64]{3,2,0,1:T(8,128)(2,1)S(1)}, u32[]{:S(2)}, u32[]{:S(2)}) collective-permute-start(bf16[2,1,80,64]{3,2,0,1:T(8,128)(2,1)S(1)} %bitcast.22), channel_id=1, source_target_pairs={{1,0},{2,1},{3,2},{4,3},{5,4},{6,5},{7,6},{8,7},{9,8},{10,9},{11,1... | collective-permute-start | bytes 61448 | tf_op jit(solution)/shard_map/ppermute | solution.py:231
  41.9 1.3 %copy-start = (bf16[3,768,256]{2,1,0:T(8,128)(2,1)S(1)}, bf16[3,768,256]{2,1,0:T(8,128)(2,1)}, u32[]{:S(2)}) copy-start(bf16[3,768,256]{2,1,0:T(8,128)(2,1)} %pad_maximum_fusion.4.w3_ref) | copy-start | bytes 3538948
  42.0 1.3 %copy-start.2 = (bf16[3,3,3,16,384]{4,3,2,1,0:T(8,128)(2,1)S(1)}, bf16[3,3,3,16,384]{4,3,2,1,0:T(8,128)(2,1)}, u32[]{:S(2)}) copy-start(bf16[3,3,3,16,384]{4,3,2,1,0:T(8,128)(2,1)} %w1_ref.1) | copy-start | bytes 995332
  42.0 1.3 %copy-start.3 = (f32[192]{0:T(256)S(1)}, f32[192]{0:T(256)}, u32[]{:S(2)}) copy-start(f32[192]{0:T(256)} %param.22) | copy-start | bytes 2308
  42.0 1.3 %copy-start.4 = (f32[192]{0:T(256)S(1)}, f32[192]{0:T(256)}, u32[]{:S(2)}) copy-start(f32[192]{0:T(256)} %param.23) | copy-start | bytes 2308
